TPU v7x, 32 devices: a whole 2x2x4 slice. The times are simulated.
32 devices in a mesh: fsdp: 8 (over y, x, core), seq: 4 (over z).
Axes of the slice: x: 2, y: 2, z: 4, core: 2. Of those that a mesh axis runs over, the one named last changes fastest.
Arguments:
- latent_in: float32 [8, 512, 1152], P('fsdp', 'seq'), may hold values from -6 to 6
- time_embed: float32 [8, 6912], P('fsdp'), may hold values from -4 to 4
- text_embed: bfloat16 [8, 120, 1152], P('fsdp'), may hold values from -6 to 6
- grad_out: float32 [8, 512, 1152], P('fsdp', 'seq'), may hold values from -6 to 6
- attn_weight: float32 [6, 1152, 1152], P(None, 'fsdp', 'seq'), may hold values from -0.1875 to 0.1875
- attn_first: float32 [6, 1152, 1152], P(None, 'fsdp', 'seq'), may hold values from -20 to 20
- attn_second: float32 [6, 1152, 1152], P(None, 'fsdp', 'seq'), may hold values from 0.4096 to 8.192
- textkv_weight: float32 [2, 1152, 1152], P(None, 'fsdp', 'seq'), may hold values from -0.1875 to 0.1875
- textkv_first: float32 [2, 1152, 1152], P(None, 'fsdp', 'seq'), may hold values from -20 to 20
- textkv_second: float32 [2, 1152, 1152], P(None, 'fsdp', 'seq'), may hold values from 0.4096 to 8.192
- mlp_weight: float32 [2, 1152, 4608], P(None, 'fsdp', 'seq'), may hold values from -0.1875 to 0.1875
- mlp_first: float32 [2, 1152, 4608], P(None, 'fsdp', 'seq'), may hold values from -20 to 20
- mlp_second: float32 [2, 1152, 4608], P(None, 'fsdp', 'seq'), may hold values from 0.4096 to 8.192
- table_weight: float32 [6912], P('seq'), may hold values from -0.4375 to 0.4375
- table_first: float32 [6912], P('seq'), may hold values from -20 to 20
- table_second: float32 [6912], P('seq'), may hold values from 0.4096 to 8.192
Outputs:
- block_out: float32 [8, 512, 1152], P('fsdp', 'seq')
- latent_grad: float32 [8, 512, 1152], P('fsdp', 'seq')
- text_grad: float32 [8, 120, 1152], P('fsdp', None, 'seq')
- time_grad: float32 [8, 6912], P('fsdp', 'seq')
- attn_grad: float32 [6, 1152, 1152], P(None, 'fsdp', 'seq')
- textkv_grad: float32 [2, 1152, 1152], P(None, 'fsdp', 'seq')
- mlp_grad: float32 [2, 1152, 4608], P(None, 'fsdp', 'seq')
- table_grad: float32 [6912], P('seq')
- attn_new: float32 [6, 1152, 1152], P(None, 'fsdp', 'seq')
- textkv_new: float32 [2, 1152, 1152], P(None, 'fsdp', 'seq')
- mlp_new: float32 [2, 1152, 4608], P(None, 'fsdp', 'seq')
- table_new: float32 [6912], P('seq')
- attn_first_new: float32 [6, 1152, 1152], P(None, 'fsdp', 'seq')
- textkv_first_new: float32 [2, 1152, 1152], P(None, 'fsdp', 'seq')
- mlp_first_new: float32 [2, 1152, 4608], P(None, 'fsdp', 'seq')
- table_first_new: float32 [6912], P('seq')
- attn_second_new: float32 [6, 1152, 1152], P(None, 'fsdp', 'seq')
- textkv_second_new: float32 [2, 1152, 1152], P(None, 'fsdp', 'seq')
- mlp_second_new: float32 [2, 1152, 4608], P(None, 'fsdp', 'seq')
- table_second_new: float32 [6912], P('seq')
All inputs are finite; a program needn't handle non-finite values.
Results may differ from a plain program's by a relative error of at most 0.025.
Values may be sent and summed in bfloat16 or wider, within the bound.
A program may use at most 192 MiB of HBM per device.

v0:
```python
import math

import jax
import jax.numpy as jnp
from jax import lax
from jax.sharding import PartitionSpec as P

HEAD_DIM = 72


norm_eps = 1e-06
gelu_coef = 0.7978845608028654
gelu_cube = 0.044715
beta_first = 0.9
beta_second = 0.999
adam_eps = 1e-08
learn_rate = 0.05
weight_decay = 0.01
fix_first = 1.0 - 0.9**10
fix_second = 1.0 - 0.999**10


def layer_norm(rows):
    centre = rows - jnp.mean(rows, axis=-1, keepdims=True)
    recip = lax.rsqrt(jnp.mean(centre * centre, axis=-1, keepdims=True) + norm_eps)
    return (centre * recip, recip)


def norm_back(grad_norm, normed, recip):
    return recip * (
        grad_norm
        - jnp.mean(grad_norm, axis=-1, keepdims=True)
        - normed * jnp.mean(grad_norm * normed, axis=-1, keepdims=True)
    )


def gelu_pair(hidden):
    inner = gelu_coef * (hidden + gelu_cube * hidden * hidden * hidden)
    tangent = jnp.tanh(inner)
    value_out = 0.5 * hidden * (1.0 + tangent)
    slope = 0.5 * (1.0 + tangent) + 0.5 * hidden * (1.0 - tangent * tangent) * gelu_coef * (
        1.0 + 3.0 * gelu_cube * hidden * hidden
    )
    return (value_out, slope)


def adamw(weight, moment, second, gradient):
    moment_new = beta_first * moment + (1.0 - beta_first) * gradient
    second_new = beta_second * second + (1.0 - beta_second) * gradient * gradient
    update = moment_new / fix_first / (jnp.sqrt(second_new / fix_second) + adam_eps)
    return (weight - learn_rate * (update + weight_decay * weight), moment_new, second_new)


def heads_forward(rows, n_seq):
    latents, tokens, mats, width = rows.shape
    group = width // n_seq
    moved = lax.all_to_all(
        rows.reshape(latents, tokens, mats, n_seq, group),
        "seq",
        split_axis=3,
        concat_axis=1,
        tiled=True,
    )
    return moved.reshape(latents, tokens * n_seq, mats, group)


def tokens_forward(heads, n_seq):
    latents, length, mats, group = heads.shape
    moved = lax.all_to_all(
        heads.reshape(latents, length, mats, 1, group),
        "seq",
        split_axis=1,
        concat_axis=3,
        tiled=True,
    )
    return moved.reshape(latents, length // n_seq, mats, n_seq * group)


def heads_backward(rows, n_seq):
    latents, tokens, mats, width = rows.shape
    group = width // n_seq
    moved = lax.all_to_all(
        rows.reshape(latents, tokens, mats, n_seq, group),
        "seq",
        split_axis=3,
        concat_axis=1,
        tiled=True,
    )
    return moved.reshape(latents, tokens * n_seq, mats, group)


def tokens_backward(heads, n_seq):
    latents, length, mats, group = heads.shape
    moved = lax.all_to_all(
        heads.reshape(latents, length, mats, 1, group),
        "seq",
        split_axis=1,
        concat_axis=3,
        tiled=True,
    )
    return moved.reshape(latents, length // n_seq, mats, n_seq * group)


def attend(query_rows, key_rows, value_rows, block):
    latents, length, group, width = query_rows.shape
    count = length // block
    pieces = jnp.moveaxis(query_rows.reshape(latents, count, block, group, width), 1, 0)

    def one_block(piece):
        scores = jnp.einsum(
            "bqgd,bkgd->bgqk", piece, key_rows, preferred_element_type=jnp.float32
        ) * width ** (-0.5)
        row_max = jnp.max(scores, axis=-1, keepdims=True)
        log_total = row_max + jnp.log(jnp.sum(jnp.exp(scores - row_max), axis=-1, keepdims=True))
        soft_b = jnp.exp(scores - log_total).astype(jnp.bfloat16)
        output = jnp.einsum(
            "bgqk,bkgd->bqgd", soft_b, value_rows, preferred_element_type=jnp.float32
        ).astype(jnp.bfloat16)
        return (output, log_total)

    outputs, totals = lax.map(one_block, pieces)
    return (jnp.moveaxis(outputs, 0, 1).reshape(query_rows.shape), totals)


def attend_back(query_rows, key_rows, value_rows, totals, grad_rows, block):
    latents, length, group, width = query_rows.shape
    count = length // block
    query_pieces = jnp.moveaxis(query_rows.reshape(latents, count, block, group, width), 1, 0)
    grad_pieces = jnp.moveaxis(grad_rows.reshape(latents, count, block, group, width), 1, 0)

    def one_block(carry, item):
        piece, grad_piece, log_total = item
        scores = jnp.einsum(
            "bqgd,bkgd->bgqk", piece, key_rows, preferred_element_type=jnp.float32
        ) * width ** (-0.5)
        soft = jnp.exp(scores - log_total)
        grad_soft = jnp.einsum(
            "bqgd,bkgd->bgqk", grad_piece, value_rows, preferred_element_type=jnp.float32
        )
        row_dot = jnp.sum(soft * grad_soft, axis=-1, keepdims=True)
        grad_score = (soft * (grad_soft - row_dot) * width ** (-0.5)).astype(jnp.bfloat16)
        grad_query = jnp.einsum(
            "bgqk,bkgd->bqgd", grad_score, key_rows, preferred_element_type=jnp.float32
        ).astype(jnp.bfloat16)
        grad_key = carry[0] + jnp.einsum(
            "bgqk,bqgd->bkgd", grad_score, piece, preferred_element_type=jnp.float32
        )
        grad_value = carry[1] + jnp.einsum(
            "bgqk,bqgd->bkgd",
            soft.astype(jnp.bfloat16),
            grad_piece,
            preferred_element_type=jnp.float32,
        )
        return ((grad_key, grad_value), grad_query)

    zeros = jnp.zeros(key_rows.shape, jnp.float32)
    (grad_key, grad_value), grad_query = lax.scan(
        one_block, (zeros, zeros), (query_pieces, grad_pieces, totals)
    )
    grad_query = jnp.moveaxis(grad_query, 0, 1).reshape(query_rows.shape)
    return (grad_query, grad_key.astype(jnp.bfloat16), grad_value.astype(jnp.bfloat16))


def body(
    latent_in,
    time_embed,
    text_embed,
    grad_out,
    attn_weight,
    attn_first,
    attn_second,
    textkv_weight,
    textkv_first,
    textkv_second,
    mlp_weight,
    mlp_first,
    mlp_second,
    table_weight,
    table_first,
    table_second,
):
    n_seq = lax.axis_size("seq")
    latents, tokens, width = latent_in.shape
    text_len = text_embed.shape[1]
    attn_cols, table_full = (
        lax.all_gather(attn_weight.astype(jnp.bfloat16), "seq", axis=2, tiled=True),
        lax.all_gather(table_weight.astype(jnp.bfloat16), "seq", axis=0, tiled=True),
    )
    attn_full, text_full, mlp_full = (
        lax.all_gather(attn_cols, "fsdp", axis=1, tiled=True),
        lax.all_gather(textkv_weight.astype(jnp.bfloat16), "fsdp", axis=1, tiled=True),
        lax.all_gather(mlp_weight.astype(jnp.bfloat16), "fsdp", axis=1, tiled=True),
    )
    length = tokens * n_seq
    group_width = width // n_seq
    group = group_width // HEAD_DIM
    block = math.gcd(length, 512)
    modulation = (time_embed + table_full.astype(jnp.float32)[None, :]).reshape(latents, 6, width)
    shift_one, scale_one, gate_one, shift_two, scale_two, gate_two = jnp.split(
        modulation, 6, axis=1
    )
    normed_one, recip_one = layer_norm(latent_in)
    mod_one = (normed_one * (1.0 + scale_one) + shift_one).astype(jnp.bfloat16)
    qkv_rows = jnp.einsum(
        "btd,sde->btse", mod_one, attn_full[0:3], preferred_element_type=jnp.float32
    ).astype(jnp.bfloat16)
    qkv_heads = heads_forward(qkv_rows, n_seq)
    query_rows = qkv_heads[:, :, 0].reshape(latents, length, group, HEAD_DIM)
    key_rows = qkv_heads[:, :, 1].reshape(latents, length, group, HEAD_DIM)
    value_rows = qkv_heads[:, :, 2].reshape(latents, length, group, HEAD_DIM)
    self_out, self_total = attend(query_rows, key_rows, value_rows, block)
    self_flat = tokens_forward(self_out.reshape(latents, length, 1, group_width), n_seq).reshape(
        latents, tokens, width
    )
    branch = jnp.einsum("btd,de->bte", self_flat, attn_full[3], preferred_element_type=jnp.float32)
    after_self = latent_in + gate_one * branch
    after_self_b = after_self.astype(jnp.bfloat16)
    cross_rows = jnp.einsum(
        "btd,de->bte", after_self_b, attn_full[4], preferred_element_type=jnp.float32
    ).astype(jnp.bfloat16)
    cross_query = heads_forward(cross_rows[:, :, None], n_seq).reshape(
        latents, length, group, HEAD_DIM
    )
    text_kv = jnp.einsum(
        "bsd,mde->bsme", text_embed, text_full, preferred_element_type=jnp.float32
    ).astype(jnp.bfloat16)
    text_keys = text_kv[:, :, 0].reshape(latents, text_len, group, HEAD_DIM)
    text_values = text_kv[:, :, 1].reshape(latents, text_len, group, HEAD_DIM)
    cross_out, cross_total = attend(cross_query, text_keys, text_values, block)
    cross_flat = tokens_forward(cross_out.reshape(latents, length, 1, group_width), n_seq).reshape(
        latents, tokens, width
    )
    after_cross = after_self + jnp.einsum(
        "btd,de->bte", cross_flat, attn_full[5], preferred_element_type=jnp.float32
    )
    normed_two, recip_two = layer_norm(after_cross)
    mod_two = (normed_two * (1.0 + scale_two) + shift_two).astype(jnp.bfloat16)
    mod_rows = lax.all_gather(mod_two, "seq", axis=1, tiled=True)
    hidden = jnp.einsum("bld,df->blf", mod_rows, mlp_full[0], preferred_element_type=jnp.float32)
    activated, slope = gelu_pair(hidden)
    activated_b = activated.astype(jnp.bfloat16)
    partial_out = jnp.einsum(
        "blf,df->bld", activated_b, mlp_full[1], preferred_element_type=jnp.float32
    )
    mlp_out = lax.psum_scatter(
        partial_out.astype(jnp.bfloat16), "seq", scatter_dimension=1, tiled=True
    ).astype(jnp.float32)
    block_out = after_cross + gate_two * mlp_out
    grad_gate_two = jnp.sum(grad_out * mlp_out, axis=1, keepdims=True)
    grad_mlp = (gate_two * grad_out).astype(jnp.bfloat16)
    grad_mlp_rows = lax.all_gather(grad_mlp, "seq", axis=1, tiled=True)
    grad_down = jnp.einsum(
        "bld,blf->df", grad_mlp_rows, activated_b, preferred_element_type=jnp.float32
    )
    grad_act = jnp.einsum(
        "bld,df->blf", grad_mlp_rows, mlp_full[1], preferred_element_type=jnp.float32
    )
    grad_hidden = (grad_act * slope).astype(jnp.bfloat16)
    grad_up = jnp.einsum("bld,blf->df", mod_rows, grad_hidden, preferred_element_type=jnp.float32)
    grad_mod_part = jnp.einsum(
        "blf,df->bld", grad_hidden, mlp_full[0], preferred_element_type=jnp.float32
    )
    grad_mod_two = lax.psum_scatter(
        grad_mod_part.astype(jnp.bfloat16), "seq", scatter_dimension=1, tiled=True
    ).astype(jnp.float32)
    grad_scale_two = jnp.sum(grad_mod_two * normed_two, axis=1, keepdims=True)
    grad_shift_two = jnp.sum(grad_mod_two, axis=1, keepdims=True)
    grad_cross = grad_out + norm_back(grad_mod_two * (1.0 + scale_two), normed_two, recip_two)
    grad_cross_b = grad_cross.astype(jnp.bfloat16)
    grad_cross_out = jnp.einsum(
        "bte,de->btd", grad_cross_b, attn_full[5], preferred_element_type=jnp.float32
    ).astype(jnp.bfloat16)
    grad_cross_heads = heads_backward(grad_cross_out[:, :, None], n_seq).reshape(
        latents, length, group, HEAD_DIM
    )
    grad_cq, grad_tk, grad_tv = attend_back(
        cross_query, text_keys, text_values, cross_total, grad_cross_heads, block
    )
    grad_cq_rows = tokens_backward(grad_cq.reshape(latents, length, 1, group_width), n_seq).reshape(
        latents, tokens, width
    )
    grad_self = grad_cross + jnp.einsum(
        "bte,de->btd", grad_cq_rows, attn_full[4], preferred_element_type=jnp.float32
    )
    grad_text_kv = jnp.stack(
        [
            grad_tk.reshape(latents, text_len, group_width),
            grad_tv.reshape(latents, text_len, group_width),
        ],
        axis=2,
    )
    grad_textkv_w = jnp.einsum(
        "bsd,bsme->mde", text_embed, grad_text_kv, preferred_element_type=jnp.float32
    )
    grad_text_part = jnp.einsum(
        "bsme,mde->bsd", grad_text_kv, text_full, preferred_element_type=jnp.float32
    )
    grad_gate_one = jnp.sum(grad_self * branch, axis=1, keepdims=True)
    grad_branch = (gate_one * grad_self).astype(jnp.bfloat16)
    grad_self_out = jnp.einsum(
        "bte,de->btd", grad_branch, attn_full[3], preferred_element_type=jnp.float32
    ).astype(jnp.bfloat16)
    grad_self_heads = heads_backward(grad_self_out[:, :, None], n_seq).reshape(
        latents, length, group, HEAD_DIM
    )
    grad_q, grad_k, grad_v = attend_back(
        query_rows, key_rows, value_rows, self_total, grad_self_heads, block
    )
    grad_qkv_heads = jnp.stack(
        [
            grad_q.reshape(latents, length, group_width),
            grad_k.reshape(latents, length, group_width),
            grad_v.reshape(latents, length, group_width),
        ],
        axis=2,
    )
    grad_qkv_rows = tokens_backward(grad_qkv_heads, n_seq)
    grad_mod_one = jnp.einsum(
        "btse,sde->btd", grad_qkv_rows, attn_full[0:3], preferred_element_type=jnp.float32
    )
    grad_scale_one = jnp.sum(grad_mod_one * normed_one, axis=1, keepdims=True)
    grad_shift_one = jnp.sum(grad_mod_one, axis=1, keepdims=True)
    latent_grad = grad_self + norm_back(grad_mod_one * (1.0 + scale_one), normed_one, recip_one)
    grad_time_part = jnp.concatenate(
        [
            grad_shift_one,
            grad_scale_one,
            grad_gate_one,
            grad_shift_two,
            grad_scale_two,
            grad_gate_two,
        ],
        axis=1,
    ).reshape(latents, 6 * width)
    grad_mlp_part = jnp.stack([grad_up, grad_down])
    grad_cproj = jnp.einsum(
        "btd,bte->de", cross_flat, grad_cross_b, preferred_element_type=jnp.float32
    )
    grad_cquery_w = jnp.einsum(
        "btd,bte->de", after_self_b, grad_cq_rows, preferred_element_type=jnp.float32
    )
    grad_proj = jnp.einsum(
        "btd,bte->de", self_flat, grad_branch, preferred_element_type=jnp.float32
    )
    grad_qkv_w = jnp.einsum(
        "btd,btse->sde", mod_one, grad_qkv_rows, preferred_element_type=jnp.float32
    )
    grad_attn_part = jnp.concatenate(
        [grad_qkv_w, grad_proj[None], grad_cquery_w[None], grad_cproj[None]], axis=0
    )
    attn_over_tokens, text_grad, time_grad = (
        lax.psum_scatter(
            grad_attn_part.astype(jnp.bfloat16), "seq", scatter_dimension=2, tiled=True
        ).astype(jnp.float32),
        lax.psum_scatter(
            grad_text_part.astype(jnp.bfloat16), "seq", scatter_dimension=2, tiled=True
        ).astype(jnp.float32),
        lax.psum_scatter(
            grad_time_part.astype(jnp.bfloat16), "seq", scatter_dimension=1, tiled=True
        ).astype(jnp.float32),
    )
    attn_grad, textkv_grad, mlp_grad = (
        lax.psum_scatter(
            attn_over_tokens.astype(jnp.bfloat16), "fsdp", scatter_dimension=1, tiled=True
        ).astype(jnp.float32),
        lax.psum_scatter(
            grad_textkv_w.astype(jnp.bfloat16), "fsdp", scatter_dimension=1, tiled=True
        ).astype(jnp.float32),
        lax.psum_scatter(
            grad_mlp_part.astype(jnp.bfloat16), "fsdp", scatter_dimension=1, tiled=True
        ).astype(jnp.float32),
    )
    table_grad = lax.psum(jnp.sum(time_grad, axis=0), "fsdp")
    attn_new, attn_first_new, attn_second_new = adamw(
        attn_weight, attn_first, attn_second, attn_grad
    )
    textkv_new, textkv_first_new, textkv_second_new = adamw(
        textkv_weight, textkv_first, textkv_second, textkv_grad
    )
    mlp_new, mlp_first_new, mlp_second_new = adamw(mlp_weight, mlp_first, mlp_second, mlp_grad)
    table_new, table_first_new, table_second_new = adamw(
        table_weight, table_first, table_second, table_grad
    )
    return (
        block_out,
        latent_grad,
        text_grad,
        time_grad,
        attn_grad,
        textkv_grad,
        mlp_grad,
        table_grad,
        attn_new,
        textkv_new,
        mlp_new,
        table_new,
        attn_first_new,
        textkv_first_new,
        mlp_first_new,
        table_first_new,
        attn_second_new,
        textkv_second_new,
        mlp_second_new,
        table_second_new,
    )


def solution(mesh):
    in_specs = (
        P("fsdp", "seq", None),
        P("fsdp", None),
        P("fsdp", None, None),
        P("fsdp", "seq", None),
        P(None, "fsdp", "seq"),
        P(None, "fsdp", "seq"),
        P(None, "fsdp", "seq"),
        P(None, "fsdp", "seq"),
        P(None, "fsdp", "seq"),
        P(None, "fsdp", "seq"),
        P(None, "fsdp", "seq"),
        P(None, "fsdp", "seq"),
        P(None, "fsdp", "seq"),
        P("seq"),
        P("seq"),
        P("seq"),
    )
    out_specs = (
        P("fsdp", "seq", None),
        P("fsdp", "seq", None),
        P("fsdp", None, "seq"),
        P("fsdp", "seq"),
        P(None, "fsdp", "seq"),
        P(None, "fsdp", "seq"),
        P(None, "fsdp", "seq"),
        P("seq"),
        P(None, "fsdp", "seq"),
        P(None, "fsdp", "seq"),
        P(None, "fsdp", "seq"),
        P("seq"),
        P(None, "fsdp", "seq"),
        P(None, "fsdp", "seq"),
        P(None, "fsdp", "seq"),
        P("seq"),
        P(None, "fsdp", "seq"),
        P(None, "fsdp", "seq"),
        P(None, "fsdp", "seq"),
        P("seq"),
    )
    return jax.shard_map(body, mesh=mesh, in_specs=in_specs, out_specs=out_specs, check_vma=False)
```

profile of v0, /device:TPU:0, one launch (start us, length us, event | category | flops | bytes accessed | tf_op | source)
XLA Modules:
  0.0 1106.5 jit_solution(4495879735321925388)
XLA Ops:
  10.5 92.2 %all-gather.7.cloned.1.call-done = bf16[6,144,1152]{1,0,2:T(8,128)(2,1)} async-done(((bf16[6,144,288]{1,0,2:T(8,128)(2,1)}), bf16[6,144,1152]{1,0,2:T(8,128)(2,1)}) %all-gather.7.cloned.1.call-update) | async-done | bytes 1990672 | tf_op jit(solution)/shard_map/all_gather | solution.py:186
  113.1 15.9 %all-reduce = bf16[6912]{0:T(1024)(128)(2,1)S(1)} all-reduce(bf16[6912]{0:T(1024)(128)(2,1)S(1)} %dynamic-update-slice), channel_id=1, replica_groups=mesh['fsdp'=8,'seq'=4] {'seq'}, use_global_device_ids=true, to_apply=%add | all-reduce | flops 6912 | bytes 27648
  129.6 64.5 %all-gather.9.cloned.1.call-done = bf16[6,1152,1152]{2,1,0:T(8,128)(2,1)} async-done(((bf16[6,144,1152]{2,1,0:T(8,128)(2,1)}), bf16[6,1152,1152]{2,1,0:T(8,128)(2,1)}) %all-gather.9.cloned.1.call-update) | async-done | bytes 15925264 | tf_op jit(solution)/shard_map/all_gather | solution.py:190
  199.8 27.0 %all_to_all.120 = bf16[1,128,3,4,288]{1,4,2,0,3:T(8,128)(2,1)S(1)} all-to-all(bf16[1,128,3,4,288]{1,4,2,0,3:T(8,128)(2,1)S(1)} %copy.192), channel_id=1, replica_groups=mesh['fsdp'=8,'seq'=4] {'seq'}, dimensions={3} | all-to-all | bytes 1769472 | tf_op jit(solution)/shard_map/all_to_all | solution.py:57
  235.9 11.9 %all_to_all.121 = bf16[4,2,18432]{2,1,0:T(2,128)(2,1)S(1)} all-to-all(bf16[4,2,18432]{2,1,0:T(2,128)(2,1)S(1)} %reshape.526), channel_id=1, replica_groups=mesh['fsdp'=8,'seq'=4] {'seq'}, dimensions={0} | all-to-all | bytes 589824 | tf_op jit(solution)/shard_map/all_to_all | solution.py:69
  276.8 11.2 %all_to_all.122 = bf16[4,2,18432]{2,1,0:T(2,128)(2,1)S(1)} all-to-all(bf16[4,2,18432]{2,1,0:T(2,128)(2,1)} %reshape.528), channel_id=1, replica_groups=mesh['fsdp'=8,'seq'=4] {'seq'}, dimensions={0} | all-to-all | bytes 589824 | tf_op jit(solution)/shard_map/all_to_all | solution.py:69
  296.1 28.5 %all-gather.13.cloned.1.call-done = bf16[1,512,1152]{2,1,0:T(8,128)(2,1)} async-done(((bf16[1,128,1152]{2,1,0:T(8,128)(2,1)}), bf16[1,512,1152]{2,1,0:T(8,128)(2,1)}) %all-gather.13.cloned.1.call-update) | async-done | bytes 1179664 | tf_op jit(solution)/shard_map/all_gather | solution.py:238
  333.5 28.4 %reduce-scatter.14.cloned.1.call-done = bf16[1,128,1152]{2,1,0:T(8,128)(2,1)} async-done(((bf16[1,512,1152]{2,1,0:T(8,128)(2,1)}), bf16[1,128,1152]{2,1,0:T(8,128)(2,1)}) %reduce-scatter.14.cloned.1.call-update) | async-done | bytes 294928 | tf_op jit(solution)/shard_map/reduce_scatter | solution.py:245
  364.1 29.1 %all-gather.17.cloned.1.call-done = bf16[1,512,1152]{2,1,0:T(8,128)(2,1)} async-done(((bf16[1,128,1152]{2,1,0:T(8,128)(2,1)}), bf16[1,512,1152]{2,1,0:T(8,128)(2,1)}) %all-gather.17.cloned.1.call-update) | async-done | bytes 1179664 | tf_op jit(solution)/shard_map/all_gather | solution.py:251
  404.1 28.5 %reduce-scatter.16.cloned.1.call-done = bf16[1,128,1152]{2,1,0:T(8,128)(2,1)} async-done(((bf16[1,512,1152]{2,1,0:T(8,128)(2,1)}), bf16[1,128,1152]{2,1,0:T(8,128)(2,1)}) %reduce-scatter.16.cloned.1.call-update) | async-done | bytes 294928 | tf_op jit(solution)/shard_map/reduce_scatter | solution.py:263
  439.1 12.0 %all_to_all.123 = bf16[1,128,1,4,288]{1,4,2,0,3:T(8,128)(2,1)S(1)} all-to-all(bf16[1,128,1,4,288]{1,4,2,0,3:T(8,128)(2,1)S(1)} %bitcast.316), channel_id=1, replica_groups=mesh['fsdp'=8,'seq'=4] {'seq'}, dimensions={3} | all-to-all | bytes 589824 | tf_op jit(solution)/shard_map/all_to_all | solution.py:82
  464.7 11.4 %all_to_all.124 = bf16[4,2,18432]{2,1,0:T(2,128)(2,1)S(1)} all-to-all(bf16[4,2,18432]{2,1,0:T(2,128)(2,1)S(1)} %reshape.530), channel_id=1, replica_groups=mesh['fsdp'=8,'seq'=4] {'seq'}, dimensions={0} | all-to-all | bytes 589824 | tf_op jit(solution)/shard_map/all_to_all | solution.py:94
  486.9 11.6 %all_to_all.125 = bf16[1,128,1,4,288]{1,4,2,0,3:T(8,128)(2,1)S(1)} all-to-all(bf16[1,128,1,4,288]{1,4,2,0,3:T(8,128)(2,1)S(1)} %bitcast.319), channel_id=1, replica_groups=mesh['fsdp'=8,'seq'=4] {'seq'}, dimensions={3} | all-to-all | bytes 589824 | tf_op jit(solution)/shard_map/all_to_all | solution.py:82
  504.5 8.8 fusion.54
  513.3 8.8 fusion.57
  545.5 26.8 %all-to-all-done.7 = bf16[1,512,3,1,288]{4,2,3,0,1:T(4,128)(2,1)S(1)} async-done(((bf16[1,512,3,1,288]{4,2,3,0,1:T(4,128)(2,1)}), bf16[1,512,3,1,288]{4,2,3,0,1:T(4,128)(2,1)S(1)}, u32[]{:S(2)}, u32[]{:S(2)}) %all-to-all-start.7) | async-done | bytes 884768 | tf_op jit(solution)/shard_map/all_to_all | solution.py:94
  627.2 226.0 %reduce-scatter.18.cloned.1.call-done = bf16[6,1152,288]{1,2,0:T(8,128)(2,1)} async-done(((bf16[6,1152,1152]{1,2,0:T(8,128)(2,1)}), bf16[6,1152,288]{1,2,0:T(8,128)(2,1)}) %reduce-scatter.18.cloned.1.call-update) | async-done | bytes 3981328 | tf_op jit(solution)/shard_map/reduce_scatter | solution.py:352
  853.2 9.4 copy.242
  862.6 10.5 reshape.511
  878.4 59.9 %all-reduce.4.cloned.1.call-done = bf16[2,1152,288]{2,0,1:T(2,128)(2,1)} async-done(((bf16[2,1152,288]{2,0,1:T(2,128)(2,1)}), bf16[2,1152,288]{2,0,1:T(2,128)(2,1)}) %all-reduce.4.cloned.1.call-update) | async-done | bytes 1327120
  940.7 37.5 %reduce-scatter.24.cloned.1.call-done = bf16[1728,1]{1,0:T(8,128)(2,1)} async-done(((bf16[6912,1]{1,0:T(8,128)(2,1)}), bf16[1728,1]{1,0:T(8,128)(2,1)}) %reduce-scatter.24.cloned.1.call-update) | async-done | bytes 3472
  980.0 13.7 %psum.7 = f32[1728]{0:T(1024)S(1)} all-reduce(f32[1728]{0:T(1024)S(1)} %get-tuple-element.249), channel_id=1, replica_groups=mesh['fsdp'=8,'seq'=4] {'fsdp'}, use_global_device_ids=true, to_apply=%region_28.29 | all-reduce | flops 1728 | bytes 13824 | tf_op jit(solution)/shard_map/psum | solution.py:373
  994.3 44.1 %reduce-scatter.20.cloned.1.call-done = bf16[2,144,1152]{2,1,0:T(8,128)(2,1)} async-done(((bf16[2,1152,1152]{2,1,0:T(8,128)(2,1)}), bf16[2,144,1152]{2,1,0:T(8,128)(2,1)}) %reduce-scatter.20.cloned.1.call-update) | async-done | bytes 663568 | tf_op jit(solution)/shard_map/reduce_scatter | solution.py:369
  1043.0 50.2 %reduce-scatter.26.cloned.1.call-done = bf16[144,1728]{1,0:T(8,128)(2,1)} async-done(((bf16[1152,1728]{1,0:T(8,128)(2,1)}), bf16[144,1728]{1,0:T(8,128)(2,1)}) %reduce-scatter.26.cloned.1.call-update) | async-done | bytes 497680
  (269 shorter events, 221.9 us)
Async XLA Ops:
  7.2 253.2 %copy-start = (bf16[1,120,1152]{2,1,0:T(8,128)(2,1)S(1)}, bf16[1,120,1152]{2,1,0:T(8,128)(2,1)}, u32[]{:S(2)}) copy-start(bf16[1,120,1152]{2,1,0:T(8,128)(2,1)} %param.18) | copy-start | bytes 829444
  7.2 95.5 %all-gather.7.cloned.1.call-start = ((), (), s32[]{:S(2)}) async-start(), calls=%async_computation.15 | async-start | bytes 5898240 | tf_op jit(solution)/shard_map/all_gather | solution.py:186
  10.5 98.8 %copy-start.24 = (f32[2,144,288]{2,1,0:T(8,128)S(1)}, f32[2,144,288]{2,1,0:T(8,128)}, u32[]{:S(2)}) copy-start(f32[2,144,288]{2,1,0:T(8,128)} %param.23) | copy-start | bytes 995332
  10.5 183.6 %all-gather.9.cloned.1.call-start = ((), (), s32[]{:S(2)}) async-start(), calls=%async_computation.16 | async-start | bytes 17915904 | tf_op jit(solution)/shard_map/all_gather | solution.py:190
  109.2 151.2 %all-gather.11.cloned.1.call-start = ((), (), s32[]{:S(2)}) async-start(), calls=%async_computation.17 | async-start | bytes 1990656 | tf_op jit(solution)/shard_map/all_gather | solution.py:191
  110.0 186.1 %all-gather.15.cloned.1.call-start = ((), (), s32[]{:S(2)}) async-start(), calls=%async_computation.19 | async-start | bytes 5971968 | tf_op jit(solution)/shard_map/all_gather | solution.py:192
  129.6 69.2 %copy-start.41 = (f32[128]{0:T(128)}, f32[128]{0:T(128)S(1)}, u32[]{:S(2)}) copy-start(f32[128]{0:T(128)S(1)} %add_rsqrt_fusion.1) | copy-start | bytes 1540
  256.9 11.7 %all-to-all-start.2 = ((bf16[1,128,1,4,288]{1,4,2,0,3:T(8,128)(2,1)}), bf16[1,128,1,4,288]{1,4,2,0,3:T(8,128)(2,1)S(1)}, u32[]{:S(2)}, u32[]{:S(2)}) async-start(bf16[1,128,1,4,288]{1,4,2,0,3:T(8,128)(2,1)} %bitcast.23), calls=%async_computation.2 | async-start | bytes 589824 | tf_op jit(solution)/shard_map/all_to_all | solution.py:57
  260.4 64.3 %all-gather.13.cloned.1.call-start = ((), (), s32[]{:S(2)}) async-start(), calls=%async_computation.18 | async-start | bytes 1474560 | tf_op jit(solution)/shard_map/all_gather | solution.py:238
  296.0 65.9 %reduce-scatter.14.cloned.1.call-start = ((), (), s32[]{:S(2)}) async-start(), calls=%async_computation.20 | async-start | bytes 1474560 | tf_op jit(solution)/shard_map/reduce_scatter | solution.py:245
  333.4 59.8 %all-gather.17.cloned.1.call-start = ((), (), s32[]{:S(2)}) async-start(), calls=%async_computation.21 | async-start | bytes 1474560 | tf_op jit(solution)/shard_map/all_gather | solution.py:251
  363.7 68.9 %reduce-scatter.16.cloned.1.call-start = ((), (), s32[]{:S(2)}) async-start(), calls=%async_computation.22 | async-start | bytes 1474560 | tf_op jit(solution)/shard_map/reduce_scatter | solution.py:263
  533.2 39.0 %all-to-all-start.7 = ((bf16[1,512,3,1,288]{4,2,3,0,1:T(4,128)(2,1)}), bf16[1,512,3,1,288]{4,2,3,0,1:T(4,128)(2,1)S(1)}, u32[]{:S(2)}, u32[]{:S(2)}) async-start(bf16[1,512,3,1,288]{4,2,3,0,1:T(4,128)(2,1)} %maximum_bitcast_fusion), calls=%async_computation.9 | async-start | bytes 3145728 | tf_op jit(solution)/shard_map/all_to_all | solution.py:94
  536.8 316.4 %reduce-scatter.18.cloned.1.call-start = ((), (), s32[]{:S(2)}) async-start(), calls=%async_computation.23 | async-start | bytes 19906560 | tf_op jit(solution)/shard_map/reduce_scatter | solution.py:352
  586.6 290.0 %reduce-scatter.22.cloned.1.call-start = ((), (), s32[]{:S(2)}) async-start(), calls=%async_computation.25 | async-start | bytes 368640
  598.3 340.0 %all-reduce.4.cloned.1.call-start = ((), (), s32[]{:S(2)}) async-start(), calls=%async_computation.28 | async-start | bytes 3538944
  611.4 366.8 %reduce-scatter.24.cloned.1.call-start = ((), (), s32[]{:S(2)}) async-start(), calls=%async_computation.26 | async-start | bytes 2211840
  621.6 416.8 %reduce-scatter.20.cloned.1.call-start = ((), (), s32[]{:S(2)}) async-start(), calls=%async_computation.24 | async-start | bytes 5971968 | tf_op jit(solution)/shard_map/reduce_scatter | solution.py:369
  627.1 466.1 %reduce-scatter.26.cloned.1.call-start = ((), (), s32[]{:S(2)}) async-start(), calls=%async_computation.27 | async-start | bytes 4644864
  873.1 66.3 %copy-start.35 = (f32[2,144,288]{2,1,0:T(8,128)S(1)}, f32[2,144,288]{2,1,0:T(8,128)}, u32[]{:S(2)}) copy-start(f32[2,144,288]{2,1,0:T(8,128)} %param.25) | copy-start | bytes 995332
  877.5 116.2 %copy-start.39 = (f32[1728]{0:T(1024)S(1)}, f32[1728]{0:T(1024)}, u32[]{:S(2)}) copy-start(f32[1728]{0:T(1024)} %param.30) | copy-start | bytes 20740
  877.5 116.2 %copy-start.40 = (f32[1728]{0:T(1024)S(1)}, f32[1728]{0:T(1024)}, u32[]{:S(2)}) copy-start(f32[1728]{0:T(1024)} %param.31) | copy-start | bytes 20740
  877.5 160.9 %copy-start.14 = (f32[2,144,1152]{2,1,0:T(8,128)S(1)}, f32[2,144,1152]{2,1,0:T(8,128)}, u32[]{:S(2)}) copy-start(f32[2,144,1152]{2,1,0:T(8,128)} %param.26) | copy-start | bytes 3981316
  994.3 100.8 %copy-start.8 = (f32[6,144,288]{2,1,0:T(8,128)S(1)}, f32[6,144,288]{2,1,0:T(8,128)}, u32[]{:S(2)}) copy-start(f32[6,144,288]{2,1,0:T(8,128)} %param.20) | copy-start | bytes 2985988
  (42 other events, 535.2 us)
Sparse Core Ops, SparseCore 0:
  10.6 92.0 all-gather.6
  109.3 84.7 all-gather.8
  196.6 26.5 all-gather.10
  225.4 41.3 all-gather.14
  296.2 28.4 all-gather.12
  333.5 28.2 reduce-scatter.13
  364.0 29.1 all-gather.16
  404.2 28.2 reduce-scatter.15
  586.7 266.4 reduce-scatter.17
  856.0 20.4 reduce-scatter.21
  880.2 58.0 all-reduce.3
  940.5 37.6 reduce-scatter.23
  982.1 56.3 reduce-scatter.19
  1042.1 51.0 reduce-scatter.25
where the time goes:
time: 1120 us; the launch traced here: 1110 us
  waiting for transfers between devices  723 us (65%)
  blocking collectives  115 us (10%)
  matrix products  102 us (9%)
  local copies, waits for them, and re-layouts  88.2 us (8%)
  other arithmetic  53.3 us (5%)
  between operations  16.7 us (1%)
    reduce_scatter x1, waiting for transfers between devices, body(): lax.psum_scatter(grad_attn_part.astype(jnp.bfloat16), 'seq', scatter_dime...  226 us
    unnamed x18, waiting for transfers between devices  149 us
    all_gather x1, waiting for transfers between devices, body(): lax.all_gather(attn_weight.astype(jnp.bfloat16), 'seq', axis=2, tiled=True)  92.2 us
    all_gather x1, waiting for transfers between devices, body(): lax.all_gather(attn_cols, 'fsdp', axis=1, tiled=True)  64.5 us
    unnamed x124, local copies, waits for them, and re-layouts  47.3 us
    reduce_scatter x1, waiting for transfers between devices, body(): lax.psum_scatter(grad_mlp_part.astype(jnp.bfloat16), 'fsdp', scatter_dime...  44.1 us
    all_gather x1, waiting for transfers between devices, body(): grad_mlp_rows = lax.all_gather(grad_mlp, 'seq', axis=1, tiled=True)  29.1 us
    all_gather x1, waiting for transfers between devices, body(): mod_rows = lax.all_gather(mod_two, 'seq', axis=1, tiled=True)  28.5 us
  transfers between devices with their start and end apart: 16, of which 14 were waited for; matrix products, arithmetic and copies ran while one was open for 11% of the time, Pallas kernels for 0%

commit v1 on v0

v1 whole, which is shorter than its diff:
```python
import functools
import math

import jax
import jax.numpy as jnp
from jax import lax
from jax.experimental import pallas as pl
from jax.experimental.pallas import tpu as pltpu
from jax.sharding import PartitionSpec as P

HEAD_DIM = 72


norm_eps = 1e-06
gelu_coef = 0.7978845608028654
gelu_cube = 0.044715
beta_first = 0.9
beta_second = 0.999
adam_eps = 1e-08
learn_rate = 0.05
weight_decay = 0.01
fix_first = 1.0 - 0.9**10
fix_second = 1.0 - 0.999**10


def layer_norm(rows):
    centre = rows - jnp.mean(rows, axis=-1, keepdims=True)
    recip = lax.rsqrt(jnp.mean(centre * centre, axis=-1, keepdims=True) + norm_eps)
    return (centre * recip, recip)


def norm_back(grad_norm, normed, recip):
    return recip * (
        grad_norm
        - jnp.mean(grad_norm, axis=-1, keepdims=True)
        - normed * jnp.mean(grad_norm * normed, axis=-1, keepdims=True)
    )


def gelu_pair(hidden):
    inner = gelu_coef * (hidden + gelu_cube * hidden * hidden * hidden)
    tangent = jnp.tanh(inner)
    value_out = 0.5 * hidden * (1.0 + tangent)
    slope = 0.5 * (1.0 + tangent) + 0.5 * hidden * (1.0 - tangent * tangent) * gelu_coef * (
        1.0 + 3.0 * gelu_cube * hidden * hidden
    )
    return (value_out, slope)


def adamw(weight, moment, second, gradient):
    moment_new = beta_first * moment + (1.0 - beta_first) * gradient
    second_new = beta_second * second + (1.0 - beta_second) * gradient * gradient
    update = moment_new / fix_first / (jnp.sqrt(second_new / fix_second) + adam_eps)
    return (weight - learn_rate * (update + weight_decay * weight), moment_new, second_new)


def line_gather_kernel(n, count, *refs):
    sources, targets = refs[:count], refs[count : 2 * count]
    local_sem, send_right, recv_right, send_left, recv_left = refs[2 * count :]
    me = lax.axis_index("seq")
    barrier = pltpu.get_barrier_semaphore()

    @pl.when(me > 0)
    def _():
        pl.semaphore_signal(barrier, inc=1, device_id={"seq": me - 1})

    @pl.when(me < n - 1)
    def _():
        pl.semaphore_signal(barrier, inc=1, device_id={"seq": me + 1})

    own = [
        pltpu.make_async_copy(source, target.at[me], local_sem.at[item])
        for item, (source, target) in enumerate(zip(sources, targets))
    ]
    for copy in own:
        copy.start()

    pl.semaphore_wait(barrier, jnp.where(me > 0, 1, 0) + jnp.where(me < n - 1, 1, 0))

    def hop(item, step, right):
        block = me - step if right else me + step
        source = sources[item] if step == 0 else targets[item].at[block]
        sends, receives = (send_right, recv_right) if right else (send_left, recv_left)
        return pltpu.make_async_remote_copy(
            src_ref=source,
            dst_ref=targets[item].at[block],
            send_sem=sends.at[item, step],
            recv_sem=receives.at[item, step],
            device_id={"seq": me + 1 if right else me - 1},
        )

    def arrival(item, step, right):
        block = me - 1 - step if right else me + 1 + step
        sends, receives = (send_right, recv_right) if right else (send_left, recv_left)
        return pltpu.make_async_copy(
            sources[item], targets[item].at[block], receives.at[item, step]
        )

    def sends_right(step):
        return jnp.logical_and(me - step >= 0, me < n - 1)

    def sends_left(step):
        return jnp.logical_and(me + step < n, me > 0)

    for step in range(n - 1):
        for item in range(count):

            @pl.when(sends_right(step))
            def _():
                hop(item, step, True).start()

            @pl.when(sends_left(step))
            def _():
                hop(item, step, False).start()

        for item in range(count):

            @pl.when(me - 1 - step >= 0)
            def _():
                arrival(item, step, True).wait()

            @pl.when(me + 1 + step < n)
            def _():
                arrival(item, step, False).wait()

    for step in range(n - 1):
        for item in range(count):

            @pl.when(sends_right(step))
            def _():
                hop(item, step, True).wait_send()

            @pl.when(sends_left(step))
            def _():
                hop(item, step, False).wait_send()

    for copy in own:
        copy.wait()


def line_gather(ident, *arrays):
    n = lax.axis_size("seq")
    count = len(arrays)
    anywhere = pl.BlockSpec(memory_space=pl.ANY)
    return pl.pallas_call(
        functools.partial(line_gather_kernel, n, count),
        out_shape=[jax.ShapeDtypeStruct((n,) + a.shape, a.dtype) for a in arrays],
        in_specs=[anywhere] * count,
        out_specs=[anywhere] * count,
        scratch_shapes=[pltpu.SemaphoreType.DMA((count,))]
        + [pltpu.SemaphoreType.DMA((count, n - 1))] * 4,
        compiler_params=pltpu.CompilerParams(collective_id=ident, has_side_effects=True),
    )(*arrays)


def attend(query_rows, key_rows, value_rows, block):
    latents, length, group, width = query_rows.shape
    count = length // block
    pieces = jnp.moveaxis(query_rows.reshape(latents, count, block, group, width), 1, 0)

    def one_block(piece):
        scores = jnp.einsum(
            "bqgd,bkgd->bgqk", piece, key_rows, preferred_element_type=jnp.float32
        ) * width ** (-0.5)
        row_max = jnp.max(scores, axis=-1, keepdims=True)
        log_total = row_max + jnp.log(jnp.sum(jnp.exp(scores - row_max), axis=-1, keepdims=True))
        soft_b = jnp.exp(scores - log_total).astype(jnp.bfloat16)
        output = jnp.einsum(
            "bgqk,bkgd->bqgd", soft_b, value_rows, preferred_element_type=jnp.float32
        ).astype(jnp.bfloat16)
        return (output, log_total)

    outputs, totals = lax.map(one_block, pieces)
    return (jnp.moveaxis(outputs, 0, 1).reshape(query_rows.shape), totals)


def attend_back(query_rows, key_rows, value_rows, totals, grad_rows, block):
    latents, length, group, width = query_rows.shape
    count = length // block
    query_pieces = jnp.moveaxis(query_rows.reshape(latents, count, block, group, width), 1, 0)
    grad_pieces = jnp.moveaxis(grad_rows.reshape(latents, count, block, group, width), 1, 0)

    def one_block(carry, item):
        piece, grad_piece, log_total = item
        scores = jnp.einsum(
            "bqgd,bkgd->bgqk", piece, key_rows, preferred_element_type=jnp.float32
        ) * width ** (-0.5)
        soft = jnp.exp(scores - log_total)
        grad_soft = jnp.einsum(
            "bqgd,bkgd->bgqk", grad_piece, value_rows, preferred_element_type=jnp.float32
        )
        row_dot = jnp.sum(soft * grad_soft, axis=-1, keepdims=True)
        grad_score = (soft * (grad_soft - row_dot) * width ** (-0.5)).astype(jnp.bfloat16)
        grad_query = jnp.einsum(
            "bgqk,bkgd->bqgd", grad_score, key_rows, preferred_element_type=jnp.float32
        ).astype(jnp.bfloat16)
        grad_key = carry[0] + jnp.einsum(
            "bgqk,bqgd->bkgd", grad_score, piece, preferred_element_type=jnp.float32
        )
        grad_value = carry[1] + jnp.einsum(
            "bgqk,bqgd->bkgd",
            soft.astype(jnp.bfloat16),
            grad_piece,
            preferred_element_type=jnp.float32,
        )
        return ((grad_key, grad_value), grad_query)

    zeros = jnp.zeros(key_rows.shape, jnp.float32)
    (grad_key, grad_value), grad_query = lax.scan(
        one_block, (zeros, zeros), (query_pieces, grad_pieces, totals)
    )
    grad_query = jnp.moveaxis(grad_query, 0, 1).reshape(query_rows.shape)
    return (grad_query, grad_key.astype(jnp.bfloat16), grad_value.astype(jnp.bfloat16))


def body(
    latent_in,
    time_embed,
    text_embed,
    grad_out,
    attn_weight,
    attn_first,
    attn_second,
    textkv_weight,
    textkv_first,
    textkv_second,
    mlp_weight,
    mlp_first,
    mlp_second,
    table_weight,
    table_first,
    table_second,
):
    n_seq = lax.axis_size("seq")
    me = lax.axis_index("seq")
    latents, tokens, width = latent_in.shape
    text_len = text_embed.shape[1]
    length = tokens * n_seq
    group_width = width // n_seq
    group = group_width // HEAD_DIM
    block = math.gcd(length, 512)
    f32, bf16 = jnp.float32, jnp.bfloat16
    attn_b = attn_weight.astype(bf16)
    text_b = textkv_weight.astype(bf16)

    def dot(spec, left, right):
        return jnp.einsum(spec, left, right, preferred_element_type=f32)

    def join_tokens(blocks):
        return jnp.moveaxis(blocks, 0, 1).reshape(latents, length, blocks.shape[-1])

    def own_tokens(rows):
        return lax.dynamic_slice_in_dim(rows, me * tokens, tokens, axis=1)

    cols_full = lax.all_gather(
        jnp.concatenate([attn_b[0:3], text_b, attn_b[4:5]], axis=0), "fsdp", axis=1, tiled=True
    )
    out_pieces, latent_all, table_all = line_gather(
        0,
        jnp.stack([attn_b[3], attn_b[5]]),
        latent_in.astype(bf16),
        table_weight.astype(bf16)[None, :],
    )
    out_rows = jnp.moveaxis(out_pieces, 0, 2).reshape(2, attn_b.shape[1], width)
    out_rows, cols_full = lax.optimization_barrier((out_rows, cols_full))
    out_full = lax.all_gather(out_rows, "fsdp", axis=1, tiled=True)
    mlp_b, out_full = lax.optimization_barrier((mlp_weight.astype(bf16), out_full))
    mlp_full = lax.all_gather(mlp_b, "fsdp", axis=1, tiled=True)

    modulation = (time_embed + table_all.reshape(1, -1).astype(f32)).reshape(latents, 6, width)
    shift_one, scale_one, gate_one, shift_two, scale_two, gate_two = jnp.split(
        modulation, 6, axis=1
    )
    latent_rows = join_tokens(latent_all).astype(f32)
    normed_rows, _ = layer_norm(latent_rows)
    mod_rows_one = (normed_rows * (1.0 + scale_one) + shift_one).astype(bf16)
    qkv = dot("bld,sde->sble", mod_rows_one, cols_full[0:3]).astype(bf16)
    query_rows = qkv[0].reshape(latents, length, group, HEAD_DIM)
    key_rows = qkv[1].reshape(latents, length, group, HEAD_DIM)
    value_rows = qkv[2].reshape(latents, length, group, HEAD_DIM)
    self_out, self_total = attend(query_rows, key_rows, value_rows, block)
    self_all, grad_all, cquery_pieces = line_gather(
        1,
        self_out.reshape(latents, length, group_width),
        grad_out.astype(bf16),
        attn_b[4],
    )
    proj_rows = out_full[0].reshape(n_seq, group_width, width)
    cproj_rows = out_full[1].reshape(n_seq, group_width, width)
    branch = dot("nblc,nce->ble", self_all, proj_rows)
    after_self = latent_rows + gate_one * branch
    after_self_b = after_self.astype(bf16)
    cross_query = (
        dot("bld,de->ble", after_self_b, cols_full[5])
        .astype(bf16)
        .reshape(latents, length, group, HEAD_DIM)
    )
    text_kv = dot("bsd,mde->mbse", text_embed, cols_full[3:5]).astype(bf16)
    text_keys = text_kv[0].reshape(latents, text_len, group, HEAD_DIM)
    text_values = text_kv[1].reshape(latents, text_len, group, HEAD_DIM)
    cross_out, cross_total = attend(cross_query, text_keys, text_values, block)
    (cross_all,) = line_gather(2, cross_out.reshape(latents, length, group_width))
    cross_branch = dot("nblc,nce->ble", cross_all, cproj_rows)
    after_cross = after_self + cross_branch
    own_branch = own_tokens(branch)
    own_after = latent_in + gate_one * own_branch + own_tokens(cross_branch)
    normed_two, recip_two = layer_norm(own_after)
    normed_all, _ = layer_norm(after_cross)
    mod_rows = (normed_all * (1.0 + scale_two) + shift_two).astype(bf16)
    hidden = dot("bld,df->blf", mod_rows, mlp_full[0])
    activated, slope = gelu_pair(hidden)
    activated_b = activated.astype(bf16)
    grad_mlp_rows = (gate_two * join_tokens(grad_all).astype(f32)).astype(bf16)
    grad_act = dot("bld,df->blf", grad_mlp_rows, mlp_full[1])
    grad_hidden = (grad_act * slope).astype(bf16)
    grad_mod_part = dot("blf,df->bld", grad_hidden, mlp_full[0])
    grad_mod_two = lax.psum_scatter(
        grad_mod_part.astype(bf16), "seq", scatter_dimension=1, tiled=True
    ).astype(f32)
    grad_down = dot("bld,blf->df", grad_mlp_rows, activated_b)
    grad_up = dot("bld,blf->df", mod_rows, grad_hidden)
    partial_out = dot("blf,df->bld", activated_b, mlp_full[1]).astype(bf16)
    grad_mlp_part = jnp.stack([grad_up.astype(bf16), grad_down.astype(bf16)])
    grad_mod_two, partial_out, grad_mlp_part, cquery_pieces = lax.optimization_barrier(
        (grad_mod_two, partial_out, grad_mlp_part, cquery_pieces)
    )
    cquery_full = lax.all_gather(cquery_pieces, "fsdp", axis=1, tiled=True)
    grad_scale_two = jnp.sum(grad_mod_two * normed_two, axis=1, keepdims=True)
    grad_shift_two = jnp.sum(grad_mod_two, axis=1, keepdims=True)
    grad_cross = grad_out + norm_back(grad_mod_two * (1.0 + scale_two), normed_two, recip_two)
    (grad_cross_all,) = line_gather(3, grad_cross.astype(bf16))
    grad_cross_b = join_tokens(grad_cross_all)
    own_cproj = lax.dynamic_index_in_dim(cproj_rows, me, axis=0, keepdims=False)
    own_proj = lax.dynamic_index_in_dim(proj_rows, me, axis=0, keepdims=False)
    grad_cross_heads = (
        dot("ble,ce->blc", grad_cross_b, own_cproj)
        .astype(bf16)
        .reshape(latents, length, group, HEAD_DIM)
    )
    grad_cq, grad_tk, grad_tv = attend_back(
        cross_query, text_keys, text_values, cross_total, grad_cross_heads, block
    )
    grad_cq = grad_cq.reshape(latents, length, group_width)
    grad_cq_blocks = lax.all_to_all(
        jnp.moveaxis(grad_cq.reshape(latents, n_seq, tokens, group_width), 1, 0),
        "seq",
        split_axis=0,
        concat_axis=0,
        tiled=True,
    )
    cquery_full, grad_mlp_part, partial_out = lax.optimization_barrier(
        (cquery_full, grad_mlp_part, partial_out)
    )
    mlp_grad = lax.psum_scatter(
        grad_mlp_part, "fsdp", scatter_dimension=1, tiled=True
    ).astype(f32)
    mlp_out = lax.psum_scatter(partial_out, "seq", scatter_dimension=1, tiled=True).astype(f32)
    grad_self = grad_cross + dot("nbtc,ndc->btd", grad_cq_blocks, cquery_full)
    block_out = own_after + gate_two * mlp_out
    grad_gate_two = jnp.sum(grad_out * mlp_out, axis=1, keepdims=True)
    grad_gate_one = jnp.sum(grad_self * own_branch, axis=1, keepdims=True)
    (grad_branch_all,) = line_gather(4, (gate_one * grad_self).astype(bf16))
    grad_branch = join_tokens(grad_branch_all)
    grad_self_heads = (
        dot("ble,ce->blc", grad_branch, own_proj)
        .astype(bf16)
        .reshape(latents, length, group, HEAD_DIM)
    )
    grad_q, grad_k, grad_v = attend_back(
        query_rows, key_rows, value_rows, self_total, grad_self_heads, block
    )
    grad_qkv = jnp.stack([item.reshape(latents, length, group_width) for item in (grad_q, grad_k, grad_v)])
    grad_mod_one_part = dot("sble,sde->bld", grad_qkv, cols_full[0:3])
    grad_tk = grad_tk.reshape(latents, text_len, group_width)
    grad_tv = grad_tv.reshape(latents, text_len, group_width)
    grad_text_kv = jnp.stack([grad_tk, grad_tv])
    grad_text_part = dot("mbse,mde->bsd", grad_text_kv, cols_full[3:5])
    grad_scale_one = jnp.sum(grad_mod_one_part * normed_rows, axis=1, keepdims=True)
    grad_shift_one = jnp.sum(grad_mod_one_part, axis=1, keepdims=True)
    grad_time_part = jnp.concatenate(
        [
            grad_shift_one,
            grad_scale_one,
            grad_gate_one,
            grad_shift_two,
            grad_scale_two,
            grad_gate_two,
        ],
        axis=1,
    ).reshape(latents, 6 * width)
    time_width = 6 * width // n_seq
    time_rows = -(-time_width // width)
    text_rows = text_len * group_width // width
    text_blocks = jnp.moveaxis(
        grad_text_part.astype(bf16).reshape(latents, text_len, n_seq, group_width), 2, 1
    ).reshape(latents, n_seq, text_rows, width)
    time_blocks = jnp.pad(
        grad_time_part.astype(bf16).reshape(latents, n_seq, time_width),
        ((0, 0), (0, 0), (0, time_rows * width - time_width)),
    ).reshape(latents, n_seq, time_rows, width)
    packed = jnp.concatenate(
        [
            grad_mod_one_part.astype(bf16).reshape(latents, n_seq, tokens, width),
            text_blocks,
            time_blocks,
        ],
        axis=2,
    ).reshape(latents, n_seq * (tokens + text_rows + time_rows), width)
    summed = lax.psum_scatter(packed, "seq", scatter_dimension=1, tiled=True).astype(f32)
    grad_mod_one = summed[:, :tokens]
    text_grad = summed[:, tokens : tokens + text_rows].reshape(latents, text_len, group_width)
    time_grad = summed[:, tokens + text_rows :].reshape(latents, time_rows * width)[:, :time_width]
    normed_one, recip_one = layer_norm(latent_in)
    latent_grad = grad_self + norm_back(grad_mod_one * (1.0 + scale_one), normed_one, recip_one)

    def own_cols(rows):
        return lax.dynamic_slice_in_dim(rows, me * group_width, group_width, axis=2)

    grad_cproj = dot("nblc,ble->nce", cross_all, own_cols(grad_cross_b)).reshape(width, group_width)
    grad_cquery_w = dot("bld,ble->de", after_self_b, grad_cq)
    grad_textkv_w = dot("bsd,mbse->mde", text_embed, grad_text_kv)
    grad_proj = dot("nblc,ble->nce", self_all, own_cols(grad_branch)).reshape(width, group_width)

    def reduce_rows(mats):
        part = jnp.concatenate([item.astype(bf16) for item in mats], axis=1)
        return lax.psum_scatter(part, "fsdp", scatter_dimension=0, tiled=True)

    def split_cols(rows, count):
        return jnp.moveaxis(rows.reshape(rows.shape[0], count, group_width), 1, 0)

    cross_sum = reduce_rows([grad_textkv_w[0], grad_textkv_w[1], grad_cquery_w, grad_cproj])
    cross_sum, grad_qkv, grad_proj = lax.optimization_barrier((cross_sum, grad_qkv, grad_proj))
    grad_qkv_w = dot("bld,sble->sde", mod_rows_one, grad_qkv)
    self_sum = reduce_rows([grad_qkv_w[0], grad_qkv_w[1], grad_qkv_w[2], grad_proj])
    cross_sum, self_sum = split_cols(cross_sum, 4), split_cols(self_sum, 4)
    textkv_grad = cross_sum[0:2].astype(f32)
    attn_grad = jnp.concatenate([self_sum, cross_sum[2:4]], axis=0).astype(f32)
    table_grad = lax.psum(jnp.sum(time_grad, axis=0), "fsdp")
    attn_new, attn_first_new, attn_second_new = adamw(
        attn_weight, attn_first, attn_second, attn_grad
    )
    textkv_new, textkv_first_new, textkv_second_new = adamw(
        textkv_weight, textkv_first, textkv_second, textkv_grad
    )
    mlp_new, mlp_first_new, mlp_second_new = adamw(mlp_weight, mlp_first, mlp_second, mlp_grad)
    table_new, table_first_new, table_second_new = adamw(
        table_weight, table_first, table_second, table_grad
    )
    return (
        block_out,
        latent_grad,
        text_grad,
        time_grad,
        attn_grad,
        textkv_grad,
        mlp_grad,
        table_grad,
        attn_new,
        textkv_new,
        mlp_new,
        table_new,
        attn_first_new,
        textkv_first_new,
        mlp_first_new,
        table_first_new,
        attn_second_new,
        textkv_second_new,
        mlp_second_new,
        table_second_new,
    )


def solution(mesh):
    in_specs = (
        P("fsdp", "seq", None),
        P("fsdp", None),
        P("fsdp", None, None),
        P("fsdp", "seq", None),
        P(None, "fsdp", "seq"),
        P(None, "fsdp", "seq"),
        P(None, "fsdp", "seq"),
        P(None, "fsdp", "seq"),
        P(None, "fsdp", "seq"),
        P(None, "fsdp", "seq"),
        P(None, "fsdp", "seq"),
        P(None, "fsdp", "seq"),
        P(None, "fsdp", "seq"),
        P("seq"),
        P("seq"),
        P("seq"),
    )
    out_specs = (
        P("fsdp", "seq", None),
        P("fsdp", "seq", None),
        P("fsdp", None, "seq"),
        P("fsdp", "seq"),
        P(None, "fsdp", "seq"),
        P(None, "fsdp", "seq"),
        P(None, "fsdp", "seq"),
        P("seq"),
        P(None, "fsdp", "seq"),
        P(None, "fsdp", "seq"),
        P(None, "fsdp", "seq"),
        P("seq"),
        P(None, "fsdp", "seq"),
        P(None, "fsdp", "seq"),
        P(None, "fsdp", "seq"),
        P("seq"),
        P(None, "fsdp", "seq"),
        P(None, "fsdp", "seq"),
        P(None, "fsdp", "seq"),
        P("seq"),
    )
    return jax.shard_map(body, mesh=mesh, in_specs=in_specs, out_specs=out_specs, check_vma=False)
```

time: 1120 us -> 611 us (0.55)
  waiting for transfers between devices: 723 us -> 198 us
  Pallas kernels: 0 us -> 172 us
  blocking collectives: 115 us -> 13.7 us
  local copies, waits for them, and re-layouts: 88.2 us -> 43.8 us
    reduce_scatter x4, waiting for transfers between devices: 327 us -> 81 us  [the longest x1 36.9 us: body(): lax.psum_scatter(grad_mlp_part, 'fsdp', scatter_dimension=1, tiled=True)]
    pallas_call x0 -> x5, Pallas kernels: none -> 172 us  [line_gather(): pl.pallas_call(functools.partial(line_gather_kernel, n, count), out_shape...]
    all_gather x6 -> x4, waiting for transfers between devices: 214 us -> 71.5 us  [the longest x1 38.7 us: body(): out_full = lax.all_gather(out_rows, 'fsdp', axis=1, tiled=True)]
    unnamed x18 -> x12, waiting for transfers between devices: 149 us -> 43.8 us
    all_to_all x6 -> x0, blocking collectives: 85.2 us -> none  [the longest x1 27 us: heads_forward(): lax.all_to_all(rows.reshape(latents, tokens, mats, n_seq, group), 'seq',...]
    all_to_all x2 -> x1, waiting for transfers between devices: 32.6 us -> 1.18 us  [body(): lax.all_to_all(jnp.moveaxis(grad_cq.reshape(latents, n_seq, tokens, group...]
    unnamed x124 -> x132, local copies, waits for them, and re-layouts: 47.3 us -> 18.8 us
    unnamed x1 -> x0, blocking collectives: 15.9 us -> none
  transfers between devices with their start and end apart: 16 -> 11, of which waited for: 14 -> 8; matrix products, arithmetic and copies ran while one was open for 11% -> 24% of each run, Pallas kernels for 0% -> 25%
where the time goes in v1:
time: 611 us; the launch traced here: 604 us
  waiting for transfers between devices  198 us (32%)
  Pallas kernels  172 us (28%)
  matrix products  96.7 us (16%)
  other arithmetic  59.4 us (10%)
  local copies, waits for them, and re-layouts  43.8 us (7%)
  between operations  15.4 us (3%)
  blocking collectives  13.7 us (2%)
    pallas_call x5, Pallas kernels, line_gather(): pl.pallas_call(functools.partial(line_gather_kernel, n, count), out_shape...  172 us
    dot_general x21, matrix products, dot(): return jnp.einsum(spec, left, right, preferred_element_type=f32)  64 us
    unnamed x12, waiting for transfers between devices  43.8 us
    all_gather x1, waiting for transfers between devices, body(): out_full = lax.all_gather(out_rows, 'fsdp', axis=1, tiled=True)  38.7 us
    reduce_scatter x1, waiting for transfers between devices, body(): lax.psum_scatter(grad_mlp_part, 'fsdp', scatter_dimension=1, tiled=True)  36.9 us
    all_gather x1, waiting for transfers between devices, body(): cquery_full = lax.all_gather(cquery_pieces, 'fsdp', axis=1, tiled=True)  32.8 us
    reduce_scatter x1, waiting for transfers between devices, body(): lax.psum_scatter(partial_out, 'seq', scatter_dimension=1, tiled=True)  25.7 us
    unnamed x132, local copies, waits for them, and re-layouts  18.8 us
  transfers between devices with their start and end apart: 11, of which 8 were waited for; matrix products, arithmetic and copies ran while one was open for 24% of the time, Pallas kernels for 25%

profile of v1, /device:TPU:0, one launch (start us, length us, event | category | flops | bytes accessed | tf_op | source)
XLA Modules:
  0.0 603.6 jit_solution(4344857237098896841)
XLA Ops:
  13.2 41.1 %shard_map.311 = (bf16[4,2,144,288]{3,2,1,0:T(8,128)(2,1)}, bf16[4,1,128,1152]{3,2,1,0:T(8,128)(2,1)}, bf16[4,1,1728]{2,1,0:T(2,128)(2,1)}) custom-call(bf16[2,144,288]{2,1,0:T(8,128)(2,1)} %pad_maximum_fusion.6.refs_0_, bf16[1,128,1152]{2,1,0:T(8,128)(2,1)} %get-tuple-element.264.refs_1_, bf16[1,1728]{1,0:T(2,128)(2,1)} %broadcast_in_dim.67.refs_2_), custom_call_target="tpu_custom_call" | custom-call | tf_op jit(solution)/shard_map/pallas_call | solution.py:145
  60.3 38.7 %all-gather.7.cloned.1.call-done = bf16[2,1152,1152]{2,1,0:T(8,128)(2,1)} async-done(((bf16[2,144,1152]{2,1,0:T(8,128)(2,1)}), bf16[2,1152,1152]{2,1,0:T(8,128)(2,1)}) %all-gather.7.cloned.1.call-update) | async-done | bytes 5308432 | tf_op jit(solution)/shard_map/all_gather | solution.py:266
  109.8 58.5 %shard_map.312 = (bf16[4,1,512,288]{3,2,1,0:T(8,128)(2,1)}, bf16[4,1,128,1152]{3,2,1,0:T(8,128)(2,1)}, bf16[4,144,288]{2,1,0:T(8,128)(2,1)}) custom-call(bf16[1,512,288]{2,1,0:T(8,128)(2,1)} %copy.89.refs_0_, bf16[1,128,1152]{2,1,0:T(8,128)(2,1)} %convert_element_type.363.refs_1_, bf16[144,288]{1,0:T(8,128)(2,1)} %get-tuple-element.258.refs_2_), custom_call_target="tpu_custom_call" | custom-call | tf_op jit(solution)/shard_map/pallas_call | solution.py:145
  171.8 4.6 fusion.135
  185.7 27.0 %shard_map.313 = bf16[4,1,512,288]{3,2,1,0:T(8,128)(2,1)} custom-call(bf16[1,512,288]{2,1,0:T(8,128)(2,1)} %copy.92.refs_0_), custom_call_target="tpu_custom_call" | custom-call | tf_op jit(solution)/shard_map/pallas_call | solution.py:145
  212.7 6.3 %fusion.133 = (f32[512]{0:T(512)S(1)}, f32[512,1152]{1,0:T(8,128)S(1)}, f32[512,1152]{1,0:T(8,128)}) fusion(f32[512,1152]{1,0:T(8,128)} %get-tuple-element.278, f32[1152]{0:T(1024)S(1)} %get-tuple-element.223, bf16[4,1,128,1152]{3,2,1,0:T(8,128)(2,1)S(1)} %copy-done.2, bf16[4,288,1152]{2,1,0:T(8,128)(2,1)} %bitcast.285, ...), kind=kOutput, calls=%fused_computation.220 | convolution fusion | flops 1361903104 | bytes 12098048 | tf_op jit(solution)/shard_map/nblc,nce->ble/dot_general | solution.py:247
  234.1 5.1 fusion.2
  245.8 5.5 pad_maximum_fusion
  251.2 8.5 %reduce-scatter.11.cloned.1.call-done = bf16[1,128,1152]{2,1,0:T(8,128)(2,1)} async-done(((bf16[1,512,1152]{2,1,0:T(8,128)(2,1)}), bf16[1,128,1152]{2,1,0:T(8,128)(2,1)}) %reduce-scatter.11.cloned.1.call-update) | async-done | bytes 294928 | tf_op jit(solution)/shard_map/reduce_scatter | solution.py:317
  261.6 32.8 %all-gather.11.cloned.1.call-done = bf16[4,1152,288]{2,1,0:T(8,128)(2,1)} async-done(((bf16[4,144,288]{2,1,0:T(8,128)(2,1)}), bf16[4,1152,288]{2,1,0:T(8,128)(2,1)}) %all-gather.11.cloned.1.call-update) | async-done | bytes 2654224 | tf_op jit(solution)/shard_map/all_gather | solution.py:327
  300.6 25.7 %reduce-scatter.13.cloned.1.call-done = bf16[1,128,1152]{2,1,0:T(8,128)(2,1)} async-done(((bf16[1,512,1152]{2,1,0:T(8,128)(2,1)}), bf16[1,128,1152]{2,1,0:T(8,128)(2,1)}) %reduce-scatter.13.cloned.1.call-update) | async-done | bytes 294928 | tf_op jit(solution)/shard_map/reduce_scatter | solution.py:357
  329.9 23.2 %shard_map.314 = bf16[4,1,128,1152]{3,2,1,0:T(8,128)(2,1)} custom-call(bf16[1,128,1152]{2,1,0:T(8,128)(2,1)} %get-tuple-element.241.refs_0_), custom_call_target="tpu_custom_call" | custom-call | tf_op jit(solution)/shard_map/pallas_call | solution.py:145
  367.7 5.9 pad_maximum_fusion.1
  373.6 5.2 copy.124
  396.2 22.4 %shard_map.315 = bf16[4,1,128,1152]{3,2,1,0:T(8,128)(2,1)} custom-call(bf16[1,128,1152]{2,1,0:T(8,128)(2,1)} %get-tuple-element.268.refs_0_), custom_call_target="tpu_custom_call" | custom-call | tf_op jit(solution)/shard_map/pallas_call | solution.py:145
  423.5 8.1 %fusion.59 = bf16[4,72,512]{2,1,0:T(8,128)(2,1)S(1)} fusion(bf16[512,4,72]{0,2,1:T(8,128)(2,1)S(1)} %bitcast.302, f32[4,512,512]{1,2,0:T(8,128)} %fusion.141, f32[4,512,512]{1,2,0:T(8,128)} %copy-done.1, f32[4,512]{1,0:T(4,128)S(1)} %copy-done.33), kind=kOutput, calls=%fused_computation.94 | convolution fusion | flops 160582144 | bytes 8986624 | tf_op jit(solution)/shard_map/while/body/eval_jaxpr/bgqk,bkgd->bqgd/dot_general | solution.py:194
  431.7 8.2 %fusion.62 = bf16[4,72,512]{2,1,0:T(8,128)(2,1)S(1)} fusion(bf16[512,4,72]{0,2,1:T(8,128)(2,1)S(1)} %bitcast.300, f32[4,512,512]{1,2,0:T(8,128)} %fusion.141, f32[4,512,512]{1,2,0:T(8,128)} %copy-done.1, f32[4,512]{1,0:T(4,128)S(1)} %copy-done.33), kind=kOutput, calls=%fused_computation.95 | convolution fusion | flops 160582144 | bytes 8986624 | tf_op jit(solution)/shard_map/while/body/eval_jaxpr/bgqk,bqgd->bkgd/dot_general | solution.py:197
  442.9 4.9 fusion.33
  462.0 5.9 pad_maximum_fusion.2
  468.0 5.2 copy.126
  473.9 9.9 %reduce-scatter.15.cloned.1.call-done = bf16[1,160,1152]{2,1,0:T(8,128)(2,1)} async-done(((bf16[1,640,1152]{2,1,0:T(8,128)(2,1)}), bf16[1,160,1152]{2,1,0:T(8,128)(2,1)}) %reduce-scatter.15.cloned.1.call-update) | async-done | bytes 368656 | tf_op jit(solution)/shard_map/reduce_scatter | solution.py:409
  487.3 13.7 %psum.7 = f32[1728]{0:T(1024)S(1)} all-reduce(f32[1728]{0:T(1024)S(1)} %get-tuple-element.239), channel_id=1, replica_groups=mesh['fsdp'=8,'seq'=4] {'fsdp'}, use_global_device_ids=true, to_apply=%region_30.31 | all-reduce | flops 1728 | bytes 13824 | tf_op jit(solution)/shard_map/psum | solution.py:438
  506.6 36.9 %reduce-scatter.17.cloned.1.call-done = bf16[2,144,1152]{2,1,0:T(8,128)(2,1)} async-done(((bf16[2,1152,1152]{2,1,0:T(8,128)(2,1)}), bf16[2,144,1152]{2,1,0:T(8,128)(2,1)}) %reduce-scatter.17.cloned.1.call-update) | async-done | bytes 663568 | tf_op jit(solution)/shard_map/reduce_scatter | solution.py:354
  547.6 43.0 %reduce-scatter.21.cloned.1.call-done = bf16[144,1152]{1,0:T(8,128)(2,1)} async-done(((bf16[1152,1152]{1,0:T(8,128)(2,1)}), bf16[144,1152]{1,0:T(8,128)(2,1)}) %reduce-scatter.21.cloned.1.call-update) | async-done | bytes 331792
  (268 shorter events, 141.9 us)
Async XLA Ops:
  7.2 161.1 %copy-start = (bf16[1,120,1152]{2,1,0:T(8,128)(2,1)S(1)}, bf16[1,120,1152]{2,1,0:T(8,128)(2,1)}, u32[]{:S(2)}) copy-start(bf16[1,120,1152]{2,1,0:T(8,128)(2,1)} %param.18) | copy-start | bytes 829444
  7.2 50.2 %all-gather.5.cloned.1.call-start = ((), (), s32[]{:S(2)}) async-start(), calls=%async_computation.7 | async-start | bytes 5971968 | tf_op jit(solution)/shard_map/all_gather | solution.py:255
  10.5 88.5 %all-gather.7.cloned.1.call-start = ((), (), s32[]{:S(2)}) async-start(), calls=%async_computation.8 | async-start | bytes 5971968 | tf_op jit(solution)/shard_map/all_gather | solution.py:266
  57.4 41.7 %copy-start.39 = (bf16[4,1,1728]{2,1,0:T(2,128)(2,1)S(1)}, bf16[4,1,1728]{2,1,0:T(2,128)(2,1)}, u32[]{:S(2)}) copy-start(bf16[4,1,1728]{2,1,0:T(2,128)(2,1)} %get-tuple-element.130) | copy-start | bytes 41476
  57.4 41.9 %copy-start.40 = (f32[1,6912]{1,0:T(1,128)S(1)}, f32[1,6912]{1,0:T(1,128)}, u32[]{:S(2)}) copy-start(f32[1,6912]{1,0:T(1,128)} %param.17) | copy-start | bytes 82948
  57.4 42.7 %copy-start.2 = (bf16[4,1,128,1152]{3,2,1,0:T(8,128)(2,1)S(1)}, bf16[4,1,128,1152]{3,2,1,0:T(8,128)(2,1)}, u32[]{:S(2)}) copy-start(bf16[4,1,128,1152]{3,2,1,0:T(8,128)(2,1)} %get-tuple-element.133) | copy-start | bytes 3538948
  57.4 163.4 %all-gather.9.cloned.1.call-start = ((), (), s32[]{:S(2)}) async-start(), calls=%async_computation.9 | async-start | bytes 5971968 | tf_op jit(solution)/shard_map/all_gather | solution.py:268
  99.1 160.7 %reduce-scatter.11.cloned.1.call-start = ((), (), s32[]{:S(2)}) async-start(), calls=%async_computation.10 | async-start | bytes 1474560 | tf_op jit(solution)/shard_map/reduce_scatter | solution.py:317
  100.1 196.9 %copy-start.30 = (f32[1152]{0:T(1024)}, f32[1152]{0:T(1024)S(1)}, u32[]{:S(2)}) copy-start(f32[1152]{0:T(1024)S(1)} %get-tuple-element.223) | copy-start | bytes 13828
  182.7 29.9 %copy-start.35 = (f32[4,512]{1,0:T(4,128)}, f32[4,512]{1,0:T(4,128)S(1)}, u32[]{:S(2)}) copy-start(f32[4,512]{1,0:T(4,128)S(1)} %log_add_fusion) | copy-start | bytes 24580
  231.8 62.6 %all-gather.11.cloned.1.call-start = ((), (), s32[]{:S(2)}) async-start(), calls=%async_computation.11 | async-start | bytes 3981312 | tf_op jit(solution)/shard_map/all_gather | solution.py:327
  251.2 43.3 %copy-start.55 = (f32[128]{0:T(128)S(1)}, f32[128]{0:T(128)}, u32[]{:S(2)}) copy-start(f32[128]{0:T(128)} %get-tuple-element.263) | copy-start | bytes 1540
  261.6 64.8 %reduce-scatter.13.cloned.1.call-start = ((), (), s32[]{:S(2)}) async-start(), calls=%async_computation.12 | async-start | bytes 1474560 | tf_op jit(solution)/shard_map/reduce_scatter | solution.py:357
  294.4 163.4 %reduce-scatter.19.cloned.1.call-start = ((), (), s32[]{:S(2)}) async-start(), calls=%async_computation.15 | async-start | bytes 2985984
  380.6 11.2 %all-to-all-start = ((bf16[4,1,128,288]{2,3,1,0:T(8,128)(2,1)}), bf16[4,1,128,288]{2,3,1,0:T(8,128)(2,1)}, u32[]{:S(2)}, u32[]{:S(2)}) async-start(bf16[4,1,128,288]{2,3,1,0:T(8,128)(2,1)} %copy.94), calls=%async_computation.2 | async-start | bytes 589824 | tf_op jit(solution)/shard_map/all_to_all | solution.py:344
  384.7 99.1 %reduce-scatter.15.cloned.1.call-start = ((), (), s32[]{:S(2)}) async-start(), calls=%async_computation.13 | async-start | bytes 1843200 | tf_op jit(solution)/shard_map/reduce_scatter | solution.py:409
  450.7 92.8 %reduce-scatter.17.cloned.1.call-start = ((), (), s32[]{:S(2)}) async-start(), calls=%async_computation.14 | async-start | bytes 5971968 | tf_op jit(solution)/shard_map/reduce_scatter | solution.py:354
  451.5 139.2 %reduce-scatter.21.cloned.1.call-start = ((), (), s32[]{:S(2)}) async-start(), calls=%async_computation.16 | async-start | bytes 2985984
  473.2 28.0 %copy-start.50 = (f32[1728]{0:T(1024)S(1)}, f32[1728]{0:T(1024)}, u32[]{:S(2)}) copy-start(f32[1728]{0:T(1024)} %param.30) | copy-start | bytes 20740
  473.2 28.0 %copy-start.51 = (f32[1728]{0:T(1024)S(1)}, f32[1728]{0:T(1024)}, u32[]{:S(2)}) copy-start(f32[1728]{0:T(1024)} %param.31) | copy-start | bytes 20740
  473.3 28.6 %copy-start.14 = (f32[1,128,1152]{2,1,0:T(8,128)S(1)}, f32[1,128,1152]{2,1,0:T(8,128)}, u32[]{:S(2)}) copy-start(f32[1,128,1152]{2,1,0:T(8,128)} %get-tuple-element.282) | copy-start | bytes 1769476
  502.9 40.5 %copy-start.7 = (f32[2,144,1152]{2,1,0:T(8,128)S(1)}, f32[2,144,1152]{2,1,0:T(8,128)}, u32[]{:S(2)}) copy-start(f32[2,144,1152]{2,1,0:T(8,128)} %param.26) | copy-start | bytes 3981316
  503.3 40.2 %copy-start.18 = (f32[2,144,1152]{2,1,0:T(8,128)S(1)}, f32[2,144,1152]{2,1,0:T(8,128)}, u32[]{:S(2)}) copy-start(f32[2,144,1152]{2,1,0:T(8,128)} %param.27) | copy-start | bytes 3981316
  547.6 44.5 %copy-start.8 = (f32[6,144,288]{2,1,0:T(8,128)S(1)}, f32[6,144,288]{2,1,0:T(8,128)}, u32[]{:S(2)}) copy-start(f32[6,144,288]{2,1,0:T(8,128)} %param.20) | copy-start | bytes 2985988
  (50 other events, 216.6 us)
Sparse Core Ops, SparseCore 0:
  10.6 44.0 all-gather.4
  57.6 41.4 all-gather.6
  101.5 41.3 all-gather.8
  231.9 27.7 reduce-scatter.10
  261.7 32.6 all-gather.10
  297.1 29.1 reduce-scatter.12
  379.0 43.2 reduce-scatter.18
  450.8 32.9 reduce-scatter.14
  487.3 56.1 reduce-scatter.16
  546.8 43.7 reduce-scatter.20

commit v2 on v1

--- a/solution.py
+++ b/solution.py
@@ -257,15 +257,13 @@
     )
     out_pieces, latent_all, table_all = line_gather(
         0,
-        jnp.stack([attn_b[3], attn_b[5]]),
+        attn_b[3:6],
         latent_in.astype(bf16),
         table_weight.astype(bf16)[None, :],
     )
-    out_rows = jnp.moveaxis(out_pieces, 0, 2).reshape(2, attn_b.shape[1], width)
+    out_rows = jnp.moveaxis(out_pieces, 0, 2).reshape(3, attn_b.shape[1], width)
     out_rows, cols_full = lax.optimization_barrier((out_rows, cols_full))
     out_full = lax.all_gather(out_rows, "fsdp", axis=1, tiled=True)
-    mlp_b, out_full = lax.optimization_barrier((mlp_weight.astype(bf16), out_full))
-    mlp_full = lax.all_gather(mlp_b, "fsdp", axis=1, tiled=True)
 
     modulation = (time_embed + table_all.reshape(1, -1).astype(f32)).reshape(latents, 6, width)
     shift_one, scale_one, gate_one, shift_two, scale_two, gate_two = jnp.split(
@@ -279,14 +277,17 @@
     key_rows = qkv[1].reshape(latents, length, group, HEAD_DIM)
     value_rows = qkv[2].reshape(latents, length, group, HEAD_DIM)
     self_out, self_total = attend(query_rows, key_rows, value_rows, block)
-    self_all, grad_all, cquery_pieces = line_gather(
+    self_all, grad_all = line_gather(
         1,
         self_out.reshape(latents, length, group_width),
         grad_out.astype(bf16),
-        attn_b[4],
-    )
+    )
+    mlp_b, out_full, self_all = lax.optimization_barrier(
+        (mlp_weight.astype(bf16), out_full, self_all)
+    )
+    mlp_full = lax.all_gather(mlp_b, "fsdp", axis=1, tiled=True)
     proj_rows = out_full[0].reshape(n_seq, group_width, width)
-    cproj_rows = out_full[1].reshape(n_seq, group_width, width)
+    cproj_rows = out_full[2].reshape(n_seq, group_width, width)
     branch = dot("nblc,nce->ble", self_all, proj_rows)
     after_self = latent_rows + gate_one * branch
     after_self_b = after_self.astype(bf16)
@@ -319,12 +320,15 @@
     ).astype(f32)
     grad_down = dot("bld,blf->df", grad_mlp_rows, activated_b)
     grad_up = dot("bld,blf->df", mod_rows, grad_hidden)
-    partial_out = dot("blf,df->bld", activated_b, mlp_full[1]).astype(bf16)
+    partial_out = dot("blf,df->bld", activated_b, mlp_full[1])
+    grad_gate_two = jnp.sum(join_tokens(grad_all).astype(f32) * partial_out, axis=1, keepdims=True)
+    partial_out = partial_out.astype(bf16)
     grad_mlp_part = jnp.stack([grad_up.astype(bf16), grad_down.astype(bf16)])
-    grad_mod_two, partial_out, grad_mlp_part, cquery_pieces = lax.optimization_barrier(
-        (grad_mod_two, partial_out, grad_mlp_part, cquery_pieces)
-    )
-    cquery_full = lax.all_gather(cquery_pieces, "fsdp", axis=1, tiled=True)
+    grad_mod_two, partial_out, grad_mlp_part = lax.optimization_barrier(
+        (grad_mod_two, partial_out, grad_mlp_part)
+    )
+    mlp_sum = lax.psum_scatter(grad_mlp_part, "fsdp", scatter_dimension=1, tiled=True)
+    mlp_out = lax.psum_scatter(partial_out, "seq", scatter_dimension=1, tiled=True)
     grad_scale_two = jnp.sum(grad_mod_two * normed_two, axis=1, keepdims=True)
     grad_shift_two = jnp.sum(grad_mod_two, axis=1, keepdims=True)
     grad_cross = grad_out + norm_back(grad_mod_two * (1.0 + scale_two), normed_two, recip_two)
@@ -348,18 +352,11 @@
         concat_axis=0,
         tiled=True,
     )
-    cquery_full, grad_mlp_part, partial_out = lax.optimization_barrier(
-        (cquery_full, grad_mlp_part, partial_out)
-    )
-    mlp_grad = lax.psum_scatter(
-        grad_mlp_part, "fsdp", scatter_dimension=1, tiled=True
-    ).astype(f32)
-    mlp_out = lax.psum_scatter(partial_out, "seq", scatter_dimension=1, tiled=True).astype(f32)
-    grad_self = grad_cross + dot("nbtc,ndc->btd", grad_cq_blocks, cquery_full)
-    block_out = own_after + gate_two * mlp_out
-    grad_gate_two = jnp.sum(grad_out * mlp_out, axis=1, keepdims=True)
+    grad_cq_rows = jnp.moveaxis(grad_cq_blocks, 0, 2).reshape(latents, tokens, width)
+    grad_self = grad_cross + dot("bte,de->btd", grad_cq_rows, out_full[1])
     grad_gate_one = jnp.sum(grad_self * own_branch, axis=1, keepdims=True)
-    (grad_branch_all,) = line_gather(4, (gate_one * grad_self).astype(bf16))
+    own_grad, mlp_sum = lax.optimization_barrier(((gate_one * grad_self).astype(bf16), mlp_sum))
+    (grad_branch_all,) = line_gather(4, own_grad)
     grad_branch = join_tokens(grad_branch_all)
     grad_self_heads = (
         dot("ble,ce->blc", grad_branch, own_proj)
@@ -405,34 +402,42 @@
             time_blocks,
         ],
         axis=2,
-    ).reshape(latents, n_seq * (tokens + text_rows + time_rows), width)
-    summed = lax.psum_scatter(packed, "seq", scatter_dimension=1, tiled=True).astype(f32)
+    )
+
+    def own_cols(rows):
+        return lax.dynamic_slice_in_dim(rows, me * group_width, group_width, axis=2)
+
+    grad_cproj = dot("nblc,ble->nce", cross_all, own_cols(grad_cross_b)).reshape(width, group_width)
+    grad_cquery_w = dot("bld,ble->de", after_self_b, grad_cq)
+    grad_textkv_w = dot("bsd,mbse->mde", text_embed, grad_text_kv)
+    grad_proj = dot("nblc,ble->nce", self_all, own_cols(grad_branch)).reshape(width, group_width)
+
+    def join_mats(mats):
+        return jnp.concatenate([item.astype(bf16) for item in mats], axis=1)
+
+    def split_cols(rows, count):
+        return jnp.moveaxis(rows.reshape(rows.shape[0], count, group_width), 1, 0)
+
+    cross_part, mlp_sum = lax.optimization_barrier(
+        (join_mats([grad_textkv_w[0], grad_textkv_w[1], grad_cquery_w, grad_cproj]), mlp_sum)
+    )
+    cross_sum = lax.psum_scatter(cross_part, "fsdp", scatter_dimension=0, tiled=True)
+    cross_sum, grad_qkv, grad_proj = lax.optimization_barrier((cross_sum, grad_qkv, grad_proj))
+    grad_qkv_w = dot("bld,sble->sde", mod_rows_one, grad_qkv)
+    self_part = join_mats([grad_qkv_w[0], grad_qkv_w[1], grad_qkv_w[2], grad_proj])
+    self_part, packed, mlp_out = lax.optimization_barrier((self_part, packed, mlp_out))
+    block_out = own_after + gate_two * mlp_out.astype(f32)
+    self_sum = lax.psum_scatter(self_part, "fsdp", scatter_dimension=0, tiled=True)
+    summed = jnp.sum(
+        lax.all_to_all(packed, "seq", split_axis=1, concat_axis=1, tiled=True).astype(f32), axis=1
+    )
     grad_mod_one = summed[:, :tokens]
     text_grad = summed[:, tokens : tokens + text_rows].reshape(latents, text_len, group_width)
     time_grad = summed[:, tokens + text_rows :].reshape(latents, time_rows * width)[:, :time_width]
     normed_one, recip_one = layer_norm(latent_in)
     latent_grad = grad_self + norm_back(grad_mod_one * (1.0 + scale_one), normed_one, recip_one)
-
-    def own_cols(rows):
-        return lax.dynamic_slice_in_dim(rows, me * group_width, group_width, axis=2)
-
-    grad_cproj = dot("nblc,ble->nce", cross_all, own_cols(grad_cross_b)).reshape(width, group_width)
-    grad_cquery_w = dot("bld,ble->de", after_self_b, grad_cq)
-    grad_textkv_w = dot("bsd,mbse->mde", text_embed, grad_text_kv)
-    grad_proj = dot("nblc,ble->nce", self_all, own_cols(grad_branch)).reshape(width, group_width)
-
-    def reduce_rows(mats):
-        part = jnp.concatenate([item.astype(bf16) for item in mats], axis=1)
-        return lax.psum_scatter(part, "fsdp", scatter_dimension=0, tiled=True)
-
-    def split_cols(rows, count):
-        return jnp.moveaxis(rows.reshape(rows.shape[0], count, group_width), 1, 0)
-
-    cross_sum = reduce_rows([grad_textkv_w[0], grad_textkv_w[1], grad_cquery_w, grad_cproj])
-    cross_sum, grad_qkv, grad_proj = lax.optimization_barrier((cross_sum, grad_qkv, grad_proj))
-    grad_qkv_w = dot("bld,sble->sde", mod_rows_one, grad_qkv)
-    self_sum = reduce_rows([grad_qkv_w[0], grad_qkv_w[1], grad_qkv_w[2], grad_proj])
     cross_sum, self_sum = split_cols(cross_sum, 4), split_cols(self_sum, 4)
+    mlp_grad = mlp_sum.astype(f32)
     textkv_grad = cross_sum[0:2].astype(f32)
     attn_grad = jnp.concatenate([self_sum, cross_sum[2:4]], axis=0).astype(f32)
     table_grad = lax.psum(jnp.sum(time_grad, axis=0), "fsdp")

time: 611 us -> 450 us (0.74)
  waiting for transfers between devices: 198 us -> 29.8 us
  local copies, waits for them, and re-layouts: 43.8 us -> 55.5 us
    unnamed x12 -> x10, waiting for transfers between devices: 43.8 us -> 0.13 us
    all_gather x1, waiting for transfers between devices: 38.7 us -> 0.02 us  [body(): out_full = lax.all_gather(out_rows, 'fsdp', axis=1, tiled=True)]
    reduce_scatter x1, waiting for transfers between devices: 36.9 us -> 0.01 us  [body(): lax.psum_scatter(grad_mlp_part, 'fsdp', scatter_dimension=1, tiled=True)]
    all_gather x1 -> x0, waiting for transfers between devices: 32.8 us -> none  [body(): cquery_full = lax.all_gather(cquery_pieces, 'fsdp', axis=1, tiled=True)]
    reduce_scatter x1, waiting for transfers between devices: 25.7 us -> 0.01 us  [body(): lax.psum_scatter(partial_out, 'seq', scatter_dimension=1, tiled=True)]
    all_to_all x0 -> x1, waiting for transfers between devices: none -> 15.9 us  [body(): lax.all_to_all(packed, 'seq', split_axis=1, concat_axis=1, tiled=True)]
    reduce_scatter x1 -> x0, waiting for transfers between devices: 9.93 us -> none  [body(): lax.psum_scatter(packed, 'seq', scatter_dimension=1, tiled=True).astype(f32)]
    unnamed x132 -> x114, local copies, waits for them, and re-layouts: 18.8 us -> 19.9 us
  transfers between devices with their start and end apart: 11 -> 10, of which waited for: 8 -> 2; matrix products, arithmetic and copies ran while one was open for 24% -> 40% of each run, Pallas kernels for 25% -> 38%
where the time goes in v2:
time: 450 us; the launch traced here: 442 us
  Pallas kernels  167 us (37%)
  matrix products  96.2 us (21%)
  other arithmetic  56.5 us (13%)
  local copies, waits for them, and re-layouts  55.5 us (12%)
  waiting for transfers between devices  29.8 us (7%)
  between operations  15.3 us (3%)
  blocking collectives  13.1 us (3%)
  starting transfers between devices  8.77 us (2%)
    pallas_call x5, Pallas kernels, line_gather(): pl.pallas_call(functools.partial(line_gather_kernel, n, count), out_shape...  167 us
    dot_general x21, matrix products, dot(): return jnp.einsum(spec, left, right, preferred_element_type=f32)  61.5 us
    unnamed x114, local copies, waits for them, and re-layouts  19.9 us
    all_to_all x1, waiting for transfers between devices, body(): lax.all_to_all(packed, 'seq', split_axis=1, concat_axis=1, tiled=True)  15.9 us
    reduce_scatter x1, waiting for transfers between devices, body(): lax.psum_scatter(grad_mod_part.astype(bf16), 'seq', scatter_dimension=1,...  13.7 us
    sub x4, other arithmetic, adamw(): weight - learn_rate * (update + weight_decay * weight)  13.4 us
    psum x1, blocking collectives, body(): table_grad = lax.psum(jnp.sum(time_grad, axis=0), 'fsdp')  13.1 us
    concatenate x2, other arithmetic, join_mats(): return jnp.concatenate([item.astype(bf16) for item in mats], axis=1)  12 us
  transfers between devices with their start and end apart: 10, of which 2 were waited for; matrix products, arithmetic and copies ran while one was open for 40% of the time, Pallas kernels for 38%

profile of v2, /device:TPU:0, one launch (start us, length us, event | category | flops | bytes accessed | tf_op | source)
XLA Modules:
  0.0 442.1 jit_solution(4759831910458069007)
XLA Ops:
  12.6 48.2 %shard_map.311 = (bf16[4,3,144,288]{3,2,1,0:T(8,128)(2,1)}, bf16[4,1,128,1152]{3,2,1,0:T(8,128)(2,1)}, bf16[4,1,1728]{2,1,0:T(2,128)(2,1)}) custom-call(bf16[3,144,288]{2,1,0:T(8,128)(2,1)} %get-tuple-element.268.refs_0_, bf16[1,128,1152]{2,1,0:T(8,128)(2,1)} %get-tuple-element.271.refs_1_, bf16[1,1728]{1,0:T(2,128)(2,1)} %broadcast_in_dim.67.refs_2_), custom_call_target="tpu_custom_call" | custom-call | tf_op jit(solution)/shard_map/pallas_call | solution.py:145
  76.3 45.2 %shard_map.312 = (bf16[4,1,512,288]{3,2,1,0:T(8,128)(2,1)}, bf16[4,1,128,1152]{3,2,1,0:T(8,128)(2,1)}) custom-call(bf16[1,512,288]{2,1,0:T(8,128)(2,1)} %copy.86.refs_0_, bf16[1,128,1152]{2,1,0:T(8,128)(2,1)} %convert_element_type.365.refs_1_), custom_call_target="tpu_custom_call" | custom-call | tf_op jit(solution)/shard_map/pallas_call | solution.py:145
  125.3 4.6 %fusion.142 = (bf16[1,1152,1152]{2,1,0:T(8,128)(2,1)S(1)}, bf16[1,1152,1152]{2,1,0:T(8,128)(2,1)}) fusion(bf16[3,1152,1152]{2,1,0:T(8,128)(2,1)} %all-gather.6.cloned.1.call-done), kind=kLoop, calls=%fused_computation.222 | loop fusion | bytes 10616832 | tf_op jit(solution)/shard_map/slice | solution.py:289
  137.5 26.5 %shard_map.313 = bf16[4,1,512,288]{3,2,1,0:T(8,128)(2,1)} custom-call(bf16[1,512,288]{2,1,0:T(8,128)(2,1)} %copy.89.refs_0_), custom_call_target="tpu_custom_call" | custom-call | tf_op jit(solution)/shard_map/pallas_call | solution.py:145
  164.1 6.2 %fusion.140 = (f32[512]{0:T(512)S(1)}, f32[512,1152]{1,0:T(8,128)S(1)}, f32[512,1152]{1,0:T(8,128)}) fusion(f32[512,1152]{1,0:T(8,128)} %get-tuple-element.283, f32[1152]{0:T(1024)S(1)} %get-tuple-element.229, bf16[4,1,128,1152]{3,2,1,0:T(8,128)(2,1)S(1)} %copy-done.2, bf16[4,288,1152]{2,1,0:T(8,128)(2,1)} %bitcast.302, ...), kind=kOutput, calls=%fused_computation.221 | convolution fusion | flops 1361903104 | bytes 12098048 | tf_op jit(solution)/shard_map/nblc,nce->ble/dot_general | solution.py:247
  172.2 4.5 %fusion.48 = f32[512,1152]{1,0:T(8,128)S(1)} fusion(bf16[2,1152,1152]{2,1,0:T(8,128)(2,1)} %all-gather.8.cloned.1.call-done, f32[512,1152]{1,0:T(8,128)} %copy-done.12, f32[1152]{0:T(1024)S(1)} %copy-done.46, f32[1152]{0:T(1024)S(1)} %get-tuple-element.224, f32[512]{0:T(512)S(1)} %add_rsqrt_fusion, f32[512]{0:T(512)S(1)} %broadcast_multiply_fusion), kind=kOutput, calls=%fused_computation.74 | convolution fusion | flops 1361903616 | bytes 7386112 | tf_op jit(solution)/shard_map/bld,df->blf/dot_general | solution.py:247
  183.4 4.0 fusion.2
  187.4 5.8 %fusion.36 = (bf16[1152]{0:T(1024)(128)(2,1)}, bf16[1,512,1152]{2,1,0:T(8,128)(2,1)}, bf16[512,1152]{1,0:T(8,128)(2,1)S(1)}) fusion(bf16[4,1,128,1152]{3,2,1,0:T(8,128)(2,1)S(1)} %copy-done.28, f32[1152]{0:T(1024)S(1)} %get-tuple-element.226, bf16[2,1152,1152]{2,1,0:T(8,128)(2,1)} %all-gather.8.cloned.1.call-done, f32[512,1152]{1,0:T(8,128)S(1)} %copy-done.52), kind=kOutput, calls=%fused_computation.54 | convolution fusion | flops 1367800704 | bytes 8559360 | tf_op jit(solution)/shard_map/blf,df->bld/dot_general | solution.py:247
  197.9 13.7 %reduce-scatter.10.cloned.1.call-done = bf16[1,128,1152]{2,1,0:T(8,128)(2,1)} async-done(((bf16[1,512,1152]{2,1,0:T(8,128)(2,1)}), bf16[1,128,1152]{2,1,0:T(8,128)(2,1)}) %reduce-scatter.10.cloned.1.call-update) | async-done | bytes 294928 | tf_op jit(solution)/shard_map/reduce_scatter | solution.py:318
  221.0 23.2 %shard_map.314 = bf16[4,1,128,1152]{3,2,1,0:T(8,128)(2,1)} custom-call(bf16[1,128,1152]{2,1,0:T(8,128)(2,1)} %get-tuple-element.247.refs_0_), custom_call_target="tpu_custom_call" | custom-call | tf_op jit(solution)/shard_map/pallas_call | solution.py:145
  254.5 4.1 all-to-all-start
  266.1 5.9 %pad_maximum_fusion.1 = bf16[1152,1152]{0,1:T(8,128)(2,1)} fusion(bf16[1152,288]{0,1:T(8,128)(2,1)S(1)} %convolution_convert_fusion.6, bf16[1152,288]{0,1:T(8,128)(2,1)S(1)} %convolution_convert_fusion.5, bf16[1152,288]{0,1:T(8,128)(2,1)S(1)} %get-tuple-element.262, bf16[1152,288]{0,1:T(8,128)(2,1)S(1)} %get-tuple-element.261), kind=kLoop, calls=%fused_computation.32 | loop fusion | flops 10616832 | bytes 5308416 | tf_op jit(solution)/shard_map/concatenate | solution.py:416
  272.0 4.6 %fusion.90 = (bf16[1152]{0:T(1024)(128)(2,1)}, bf16[1,128,1152]{2,1,0:T(8,128)(2,1)}, f32[1,128,1152]{2,1,0:T(8,128)}) fusion(f32[512,1152]{1,0:T(8,128)} %get-tuple-element.283, s32[]{:T(128)S(6)} %select_n.13, f32[1152]{0:T(1024)S(1)} %get-tuple-element.229, f32[1,128,1152]{2,1,0:T(8,128)} %get-tuple-element.248, bf16[128,1152]{0,1:T(8,128)(2,1)} %bitcast.67, ...), kind=kOutput, calls=%fused_computation.140 | convolution fusion | flops 340474752 | bytes 5020420 | tf_op jit(solution)/shard_map/bte,de->btd/dot_general | solution.py:247
  276.6 5.2 %copy.122 = bf16[1152,1152]{1,0:T(8,128)(2,1)} copy(bf16[1152,1152]{0,1:T(8,128)(2,1)} %pad_maximum_fusion.1) | data formatting | bytes 5308416
  300.0 23.9 %shard_map.315 = bf16[4,1,128,1152]{3,2,1,0:T(8,128)(2,1)} custom-call(bf16[1,128,1152]{2,1,0:T(8,128)(2,1)} %get-tuple-element.147.refs_0_), custom_call_target="tpu_custom_call" | custom-call | tf_op jit(solution)/shard_map/pallas_call | solution.py:145
  332.4 9.1 %fusion.72 = bf16[4,72,512]{2,1,0:T(8,128)(2,1)} fusion(bf16[512,4,72]{0,2,1:T(8,128)(2,1)} %bitcast.320, f32[4,512,512]{1,2,0:T(8,128)} %fusion.149, f32[4,512,512]{1,2,0:T(8,128)} %copy-done.1, f32[4,512]{1,0:T(4,128)S(1)} %log_add_fusion.1), kind=kOutput, calls=%fused_computation.101 | convolution fusion | flops 160582144 | bytes 8986624 | tf_op jit(solution)/shard_map/while/body/eval_jaxpr/bgqk,bqgd->bkgd/dot_general | solution.py:197
  341.6 8.8 %fusion.69 = bf16[4,72,512]{2,1,0:T(8,128)(2,1)} fusion(bf16[512,4,72]{0,2,1:T(8,128)(2,1)S(1)} %bitcast.318, f32[4,512,512]{1,2,0:T(8,128)} %fusion.149, f32[4,512,512]{1,2,0:T(8,128)} %copy-done.1, f32[4,512]{1,0:T(4,128)S(1)} %log_add_fusion.1), kind=kOutput, calls=%fused_computation.100 | convolution fusion | flops 160582144 | bytes 8986624 | tf_op jit(solution)/shard_map/while/body/eval_jaxpr/bgqk,bkgd->bqgd/dot_general | solution.py:194
  350.4 5.1 %fusion.42 = (bf16[1152]{0:T(1024)(128)(2,1)S(1)}, bf16[1152]{0:T(1024)(128)(2,1)S(1)}, bf16[512,1152]{1,0:T(8,128)(2,1)}) fusion(bf16[4,1,128,1152]{3,2,1,0:T(8,128)(2,1)S(1)} %copy-done.2, f32[512]{0:T(512)} %copy-done.43, f32[512]{0:T(512)} %copy-done.41, bf16[6,1152,288]{2,1,0:T(8,128)(2,1)} %all-gather.4.cloned.1.call-done, ...), kind=kOutput, calls=%fused_computation.64 | convolution fusion | flops 1024227072 | bytes 5906944 | tf_op jit(solution)/shard_map/sble,sde->bld/dot_general | solution.py:247
  366.5 6.1 %pad_maximum_fusion.2 = bf16[1152,1152]{0,1:T(8,128)(2,1)} fusion(bf16[1152,288]{0,1:T(8,128)(2,1)S(1)} %fusion.99, bf16[1152,288]{0,1:T(8,128)(2,1)S(1)} %get-tuple-element.259, bf16[1152,288]{0,1:T(8,128)(2,1)S(1)} %get-tuple-element.260, bf16[1152,288]{0,1:T(8,128)(2,1)S(1)} %get-tuple-element.258), kind=kLoop, calls=%fused_computation.33 | loop fusion | flops 10616832 | bytes 5308416 | tf_op jit(solution)/shard_map/concatenate | solution.py:416
  376.3 5.2 %copy.124 = bf16[1152,1152]{1,0:T(8,128)(2,1)} copy(bf16[1152,1152]{0,1:T(8,128)(2,1)} %pad_maximum_fusion.2) | data formatting | bytes 5308416
  382.6 5.0 %multiply_subtract_fusion = (f32[2,144,1152]{2,1,0:T(8,128)}, f32[2,144,1152]{2,1,0:T(8,128)}, f32[2,144,1152]{2,1,0:T(8,128)}, f32[2,144,1152]{2,1,0:T(8,128)}) fusion(f32[2,144,1152]{2,1,0:T(8,128)} %param.26, f32[2,144,1152]{2,1,0:T(8,128)} %param.27, f32[2,144,1152]{2,1,0:T(8,128)} %param.28, bf16[2,144,1152]{2,1,0:T(8,128)(2,1)} %reduce-scatter.12.cloned.1.call-done), kind=kLoop, calls=%fused_computation.94 | loop fusion | flops 5308416 | bytes 9953280 | tf_op jit(solution)/shard_map/sub | solution.py:54
  392.2 15.9 %all-to-all-done.1 = bf16[1,4,160,1152]{3,2,0,1:T(8,128)(2,1)S(1)} async-done(((bf16[1,4,160,1152]{3,2,0,1:T(8,128)(2,1)}), bf16[1,4,160,1152]{3,2,0,1:T(8,128)(2,1)S(1)}, u32[]{:S(2)}, u32[]{:S(2)}) %all-to-all-start.1) | async-done | bytes 1474592 | tf_op jit(solution)/shard_map/all_to_all | solution.py:432
  411.4 13.1 %psum.7 = f32[1728]{0:T(1024)S(1)} all-reduce(f32[1728]{0:T(1024)S(1)} %get-tuple-element.245), channel_id=1, replica_groups=mesh['fsdp'=8,'seq'=4] {'fsdp'}, use_global_device_ids=true, to_apply=%region_30.31 | all-reduce | flops 1728 | bytes 13824 | tf_op jit(solution)/shard_map/psum | solution.py:443
  430.7 4.4 multiply_subtract_fusion.1
  (244 shorter events, 128.3 us)
Async XLA Ops:
  7.2 114.6 %copy-start = (bf16[1,120,1152]{2,1,0:T(8,128)(2,1)S(1)}, bf16[1,120,1152]{2,1,0:T(8,128)(2,1)}, u32[]{:S(2)}) copy-start(bf16[1,120,1152]{2,1,0:T(8,128)(2,1)} %param.18) | copy-start | bytes 829444
  7.2 57.1 %all-gather.4.cloned.1.call-start = ((), (), s32[]{:S(2)}) async-start(), calls=%async_computation.7 | async-start | bytes 5971968 | tf_op jit(solution)/shard_map/all_gather | solution.py:255
  10.6 111.0 %all-gather.6.cloned.1.call-start = ((), (), s32[]{:S(2)}) async-start(), calls=%async_computation.8 | async-start | bytes 8957952 | tf_op jit(solution)/shard_map/all_gather | solution.py:266
  64.3 107.8 %all-gather.8.cloned.1.call-start = ((), (), s32[]{:S(2)}) async-start(), calls=%async_computation.9 | async-start | bytes 5971968 | tf_op jit(solution)/shard_map/all_gather | solution.py:288
  121.6 89.9 %reduce-scatter.10.cloned.1.call-start = ((), (), s32[]{:S(2)}) async-start(), calls=%async_computation.10 | async-start | bytes 1474560 | tf_op jit(solution)/shard_map/reduce_scatter | solution.py:318
  125.3 4.6 %copy-start.17 = (bf16[4,1,512,288]{3,2,1,0:T(8,128)(2,1)S(1)}, bf16[4,1,512,288]{3,2,1,0:T(8,128)(2,1)}, u32[]{:S(2)}) copy-start(bf16[4,1,512,288]{3,2,1,0:T(8,128)(2,1)} %get-tuple-element.139) | copy-start | bytes 3538948
  172.1 4.6 %copy-start.29 = (bf16[4,1,128,1152]{3,2,1,0:T(8,128)(2,1)S(1)}, bf16[4,1,128,1152]{3,2,1,0:T(8,128)(2,1)}, u32[]{:S(2)}) copy-start(bf16[4,1,128,1152]{3,2,1,0:T(8,128)(2,1)} %fusion.34) | copy-start | bytes 3538948
  183.1 93.5 %reduce-scatter.12.cloned.1.call-start = ((), (), s32[]{:S(2)}) async-start(), calls=%async_computation.11 | async-start | bytes 5971968 | tf_op jit(solution)/shard_map/reduce_scatter | solution.py:330
  214.0 4.7 %copy-start.47 = (f32[128]{0:T(128)}, f32[128]{0:T(128)S(1)}, u32[]{:S(2)}) copy-start(f32[128]{0:T(128)S(1)} %broadcast_multiply_fusion.4) | copy-start | bytes 1540
  254.5 17.5 %all-to-all-start = ((bf16[4,1,128,288]{2,3,1,0:T(8,128)(2,1)}), bf16[4,1,128,288]{2,3,1,0:T(8,128)(2,1)}, u32[]{:S(2)}, u32[]{:S(2)}) async-start(bf16[4,1,128,288]{2,3,1,0:T(8,128)(2,1)} %copy.94), calls=%async_computation.1 | async-start | bytes 589824 | tf_op jit(solution)/shard_map/all_to_all | solution.py:348
  258.6 103.3 %reduce-scatter.16.cloned.1.call-start = ((), (), s32[]{:S(2)}) async-start(), calls=%async_computation.13 | async-start | bytes 2985984
  281.8 90.8 %reduce-scatter.14.cloned.1.call-start = ((), (), s32[]{:S(2)}) async-start(), calls=%async_computation.12 | async-start | bytes 1474560 | tf_op jit(solution)/shard_map/reduce_scatter | solution.py:331
  332.4 9.1 %copy-start.20 = (bf16[1,1,512,288]{2,3,0,1:T(8,128)(2,1)S(1)}, bf16[1,1,512,288]{2,3,0,1:T(8,128)(2,1)}, u32[]{:S(2)}) copy-start(bf16[1,1,512,288]{2,3,0,1:T(8,128)(2,1)} %copy-done.19) | copy-start | bytes 884740
  350.4 5.2 %copy-start.42 = (bf16[1,1,1152]{2,1,0:T(2,128)(2,1)S(1)}, bf16[1,1,1152]{2,1,0:T(2,128)(2,1)}, u32[]{:S(2)}) copy-start(bf16[1,1,1152]{2,1,0:T(2,128)(2,1)} %broadcast_in_dim.73) | copy-start | bytes 6916
  350.4 6.1 %copy-start.22 = (bf16[4,72,512]{2,1,0:T(8,128)(2,1)S(1)}, bf16[4,72,512]{2,1,0:T(8,128)(2,1)}, u32[]{:S(2)}) copy-start(bf16[4,72,512]{2,1,0:T(8,128)(2,1)} %convolution_convert_fusion.11) | copy-start | bytes 884740
  355.5 5.0 %copy-start.23 = (bf16[1,4,30,1152]{3,2,1,0:T(8,128)(2,1)S(1)}, bf16[1,4,30,1152]{3,2,1,0:T(8,128)(2,1)}, u32[]{:S(2)}) copy-start(bf16[1,4,30,1152]{3,2,1,0:T(8,128)(2,1)} %reshape.769) | copy-start | bytes 829444
  372.7 35.4 %all-to-all-start.1 = ((bf16[1,4,160,1152]{3,2,0,1:T(8,128)(2,1)}), bf16[1,4,160,1152]{3,2,0,1:T(8,128)(2,1)S(1)}, u32[]{:S(2)}, u32[]{:S(2)}) async-start(bf16[1,4,160,1152]{3,2,0,1:T(8,128)(2,1)} %pad_maximum_fusion.3), calls=%async_computation.4 | async-start | bytes 2949120 | tf_op jit(solution)/shard_map/all_to_all | solution.py:432
  376.2 52.9 %reduce-scatter.18.cloned.1.call-start = ((), (), s32[]{:S(2)}) async-start(), calls=%async_computation.14 | async-start | bytes 2985984
  382.6 5.0 %copy-start.13 = (bf16[144,1152]{0,1:T(8,128)(2,1)S(1)}, bf16[144,1152]{0,1:T(8,128)(2,1)}, u32[]{:S(2)}) copy-start(bf16[144,1152]{0,1:T(8,128)(2,1)} %copy.123) | copy-start | bytes 995332
  391.3 33.3 %copy-start.4 = (f32[1,128,1152]{2,1,0:T(8,128)S(1)}, f32[1,128,1152]{2,1,0:T(8,128)}, u32[]{:S(2)}) copy-start(f32[1,128,1152]{2,1,0:T(8,128)} %param.16) | copy-start | bytes 1769476
  392.2 35.2 %copy-start.11 = (f32[1,128,1152]{2,1,0:T(8,128)S(1)}, f32[1,128,1152]{2,1,0:T(8,128)}, u32[]{:S(2)}) copy-start(f32[1,128,1152]{2,1,0:T(8,128)} %get-tuple-element.287) | copy-start | bytes 1769476
  409.1 18.3 %copy-start.6 = (f32[160,1152]{1,0:T(8,128)S(1)}, f32[160,1152]{1,0:T(8,128)}, u32[]{:S(2)}) copy-start(f32[160,1152]{1,0:T(8,128)} %copy-done.5) | copy-start | bytes 2211844
  424.6 6.1 %copy-start.38 = (f32[1728]{0:T(1024)}, f32[1728]{0:T(1024)S(1)}, u32[]{:S(2)}) copy-start(f32[1728]{0:T(1024)S(1)} %psum.7) | copy-start | bytes 20740
  425.9 4.8 %copy-start.8 = (f32[6,144,288]{2,1,0:T(8,128)S(1)}, f32[6,144,288]{2,1,0:T(8,128)}, u32[]{:S(2)}) copy-start(f32[6,144,288]{2,1,0:T(8,128)} %param.20) | copy-start | bytes 2985988
  (40 other events, 99.9 us)
Sparse Core Ops, SparseCore 0:
  10.7 44.0 all-gather.3
  64.4 52.6 all-gather.5
  121.7 41.3 all-gather.7
  183.2 28.2 reduce-scatter.9
  214.9 55.9 reduce-scatter.11
  282.0 45.0 reduce-scatter.15
  330.1 29.1 reduce-scatter.13
  381.6 45.1 reduce-scatter.17
